TPU v7x, 32 devices: a whole 2x2x4 slice. The times are simulated.
32 devices in a mesh: group: 2 (over x), ctx: 16 (over z, y, core).
Axes of the slice: x: 2, y: 2, z: 4, core: 2. Of those that a mesh axis runs over, the one named last changes fastest.
Arguments:
- hyena_qkv: bfloat16 [4096, 3, 2048], P(('group', 'ctx')), parts along dimension 0, may hold values from -6 to 6
- short_weight: float32 [3, 3, 2048], replicated, may hold values from -3.5 to 3.5
- filter_rate: float32 [128, 16], replicated, as said below
- filter_residue: float32 [128, 16], replicated, may hold values from -4 to 4
- attn_qkv: bfloat16 [4096, 3, 2048], P(('group', 'ctx')), parts along dimension 0, may hold values from -6 to 6
- doc_lengths: int32 [8], P('group'), parts along dimension 0, may hold values from 1 to 897, 2048 in all
Outputs:
- hyena_out: bfloat16 [4096, 2048], P(('group', 'ctx')), parts along dimension 0
- attn_out: bfloat16 [4096, 2048], P(('group', 'ctx')), parts along dimension 0
There are 2 independent parts, one for each index of `group`. A program takes and returns all parts, laid end to end along the dimension named above; an argument that names none is the same for every part. Nothing has to cross between parts.
Inputs may be any that keep to these rules, and one draw needn't show every extreme that they name: `filter_rate`: every rate is positive and at most 1/30. `doc_lengths`: the lengths sum to 2048 and the longest is exactly 897.
All inputs are finite; a program needn't handle non-finite values.
Results may differ from a plain program's by a relative error of at most 0.0054.
Values may be sent and summed in bfloat16 or wider, within the bound.
No kernel may reach another device: no remote copies, remote signals or barrier semaphores. Data moves between devices by JAX's collectives and lax.ppermute only.
A program may use at most 128 MiB of HBM per device.

v0:
```python
import functools
import math

import jax
import jax.numpy as jnp
from jax import lax
from jax.experimental import pallas as pl
from jax.experimental.pallas import tpu as pltpu
from jax.sharding import PartitionSpec as P


HEAD = 128
LANES = 128
EDGE = 8
ROW = 4

F32 = jnp.float32
BF16 = jnp.bfloat16


def flip(value, axis, bit):
    count = lax.axis_size(axis)
    return lax.ppermute(value, axis, [(at, at ^ bit) for at in range(count)])


def side_of(at):
    return at // 2 % 2


def ahead(value, axis, steps, bit=0, first=0, side=None):
    count = lax.axis_size(axis)
    pairs = [
        (at, (at + steps) ^ bit)
        for at in range(first, count - steps)
        if side is None or side_of(at) == side
    ]
    return lax.ppermute(value, axis, pairs)


def spot():
    index = lax.axis_index("ctx")
    return index & 1, lax.shift_right_logical(index, 1) & 1, index & (ROW - 1), index // ROW


ALL_VMEM = 67043328


def limits(mib):
    return pltpu.CompilerParams(vmem_limit_bytes=mib << 20)


def cost(flops, moved, exps=0):
    return pl.CostEstimate(flops=flops, bytes_accessed=moved, transcendentals=exps)


VMEM = pl.BlockSpec(memory_space=pltpu.VMEM)
SMEM = pl.BlockSpec(memory_space=pltpu.SMEM)
ANY = pl.BlockSpec(memory_space=pl.ANY)
HBM = pl.BlockSpec(memory_space=pltpu.HBM)


def same_filter(modes, width, terms, lanes):
    row_at = lax.broadcasted_iota(jnp.int32, (terms, lanes), 0)
    lane_at = lax.broadcasted_iota(jnp.int32, (terms, lanes), 1)
    kept = None
    for g in range(terms // modes):
        both = (
            (row_at >= g * modes)
            & (row_at < (g + 1) * modes)
            & (lane_at >= g * width)
            & (lane_at < (g + 1) * width)
        )
        kept = both if kept is None else kept | both
    return kept


def feature(x, halo, w_ref, stream, at):
    here = x.astype(F32)
    halo = halo.astype(F32)
    edge = halo.shape[0]
    row_at = lax.broadcasted_iota(jnp.int32, here.shape, 0)
    one = jnp.where(row_at == 0, halo[edge - 1 :], pltpu.roll(here, 1, 0))
    two = jnp.where(row_at == 1, halo[edge - 1 :], pltpu.roll(here, 2, 0))
    two = jnp.where(row_at == 0, halo[edge - 2 : edge - 1], two)
    tap = [w_ref[n, stream : stream + 1, at] for n in range(3)]
    return tap[0] * here + tap[1] * one + tap[2] * two


def of_step(table_ref):
    groups = table_ref.shape[1]
    return pltpu.roll(table_ref[...], groups - pl.program_id(0) * (groups // STEPS), 1)


def down(table, part, filters, lanes):
    columns = [table[:, part * filters + g : part * filters + g + 1] for g in range(filters)]
    return jnp.concatenate([jnp.broadcast_to(c, (c.shape[0], lanes)) for c in columns], axis=0)


def hyena_ends_body(filters, x_ref, halo_ref, w_ref, rate_ref, mixed_ref, ends_ref, wide_ref):
    rows = x_ref.shape[1]
    modes, groups = rate_ref.shape
    parts = groups // STEPS // filters
    terms = filters * modes
    lanes = x_ref.shape[2] // parts
    width = lanes // filters
    rates = of_step(rate_ref)
    lag = (rows - 1 - lax.broadcasted_iota(jnp.int32, (terms, rows), 1)).astype(F32)
    own = same_filter(modes, width, terms, lanes)
    pick = lambda matrix: jnp.sum(jnp.where(own, matrix, 0.0).reshape(filters, modes, lanes), axis=0)
    for part in range(parts):
        at = slice(part * lanes, (part + 1) * lanes)
        key, value = (feature(x_ref[n, :, at], halo_ref[n, :, at], w_ref, n, at) for n in (1, 2))
        mixed = (key * value).astype(BF16)
        mixed_ref[:, at] = mixed
        rate = down(rates, part, filters, rows)
        powers = jnp.exp(-rate * lag)
        high = powers.astype(BF16)
        low = (powers - high.astype(F32)).astype(BF16)
        ends = jnp.dot(high, mixed, preferred_element_type=F32) + jnp.dot(
            low, mixed, preferred_element_type=F32
        )
        ends_ref[:, at] = pick(ends)
        wide_ref[:, at] = pick(rate)


STEPS = 4


def hyena_ends(streams, halo, short_weight, rates):
    _, rows, channels = streams.shape
    edge = halo.shape[1]
    modes, groups = rates.shape
    filters = groups * LANES // channels
    terms = filters * modes
    wide = channels // STEPS
    by_block = lambda n: (0, n)
    lead = lambda n: (0, 0, n)
    return pl.pallas_call(
        functools.partial(hyena_ends_body, filters),
        grid=(STEPS,),
        in_specs=[
            pl.BlockSpec((3, rows, wide), lead),
            pl.BlockSpec((3, edge, wide), lead),
            pl.BlockSpec((3, 3, wide), lead),
            pl.BlockSpec((modes, groups), lambda n: (0, 0)),
        ],
        out_specs=[
            pl.BlockSpec((rows, wide), by_block),
            pl.BlockSpec((modes, wide), by_block),
            pl.BlockSpec((modes, wide), by_block),
        ],
        out_shape=[
            jax.ShapeDtypeStruct((rows, channels), BF16),
            jax.ShapeDtypeStruct((modes, channels), F32),
            jax.ShapeDtypeStruct((modes, channels), F32),
        ],
        compiler_params=limits(16),
        cost_estimate=cost(4 * rows * terms * channels, 8 * rows * channels),
        name="hyena_ends",
    )(streams, halo, short_weight, rates)


def hyena_near_body(filters, mixed_ref, rate_ref, res_ref, near_ref, taps_s, u_s):
    rows = mixed_ref.shape[0]
    modes, groups = rate_ref.shape
    parts = groups // STEPS // filters
    terms = filters * modes
    lanes = mixed_ref.shape[1] // parts
    width = lanes // filters
    rates = of_step(rate_ref)
    coeffs = of_step(res_ref) * jnp.sqrt(2.0 * rates / modes)
    row_at = lax.broadcasted_iota(jnp.int32, (rows, lanes), 0)
    lane_at = lax.broadcasted_iota(jnp.int32, (rows, lanes), 1)
    lag = (rows - 1 - lax.broadcasted_iota(jnp.int32, (terms, rows), 1)).astype(F32)
    zero = jnp.zeros((rows, lanes), BF16)
    for part in range(parts):
        at = slice(part * lanes, (part + 1) * lanes)
        mixed = mixed_ref[:, at]
        rate = down(rates, part, filters, rows)
        powers = down(coeffs, part, filters, rows) * jnp.exp(-rate * lag)
        backward = jnp.sum(powers.reshape(filters, modes, rows), axis=1)
        for g in range(filters):
            spread = jnp.broadcast_to(backward[g : g + 1], (rows, rows))
            shifted = pltpu.roll(spread, 1, 1, stride=1, stride_axis=0)
            kept = jnp.where(lane_at <= row_at, shifted, 0.0)
            taps_s[part, :, g * rows : (g + 1) * rows] = kept.astype(BF16)
            mine = (lane_at >= g * width) & (lane_at < (g + 1) * width)
            u_s[part, g * rows : (g + 1) * rows, :] = jnp.where(mine, mixed, zero)
        near_ref[:, at] = jnp.dot(taps_s[part], u_s[part], preferred_element_type=F32)


def hyena_near(mixed, rates, residues):
    rows, channels = mixed.shape
    modes, groups = rates.shape
    lanes = LANES
    filters = groups * lanes // channels
    parts = groups // STEPS // filters
    wide = channels // STEPS
    by_block = lambda n: (0, n)
    whole = lambda n: (0, 0)
    return pl.pallas_call(
        functools.partial(hyena_near_body, filters),
        grid=(STEPS,),
        in_specs=[
            pl.BlockSpec((rows, wide), by_block),
            pl.BlockSpec((modes, groups), whole),
            pl.BlockSpec((modes, groups), whole),
        ],
        out_specs=pl.BlockSpec((rows, wide), by_block),
        out_shape=jax.ShapeDtypeStruct((rows, channels), F32),
        scratch_shapes=[
            pltpu.VMEM((parts, rows, filters * rows), BF16),
            pltpu.VMEM((parts, filters * rows, lanes), BF16),
        ],
        compiler_params=limits(16),
        cost_estimate=cost(2 * rows * rows * filters * channels, 12 * rows * channels),
        name="hyena_near",
    )(mixed, rates, residues)


def hyena_out_body(filters, near_ref, x_ref, halo_ref, w_ref, carried_ref, rate_ref, res_ref, out_ref):
    rows = near_ref.shape[0]
    modes, groups = rate_ref.shape
    parts = groups // STEPS // filters
    terms = filters * modes
    lanes = near_ref.shape[1] // parts
    width = lanes // filters
    rates = of_step(rate_ref)
    coeffs = of_step(res_ref) * jnp.sqrt(2.0 * rates / modes)
    lag = (1 + lax.broadcasted_iota(jnp.int32, (terms, rows), 1)).astype(F32)
    own = same_filter(modes, width, terms, lanes)
    for part in range(parts):
        at = slice(part * lanes, (part + 1) * lanes)
        rate = down(rates, part, filters, rows)
        powers = (down(coeffs, part, filters, rows) * jnp.exp(-rate * lag)).T
        p_high = powers.astype(BF16)
        p_low = (powers - p_high.astype(F32)).astype(BF16)
        carried = jnp.where(own, jnp.concatenate([carried_ref[:, at]] * filters, axis=0), 0.0)
        c_high = carried.astype(BF16)
        c_low = (carried - c_high.astype(F32)).astype(BF16)
        far = (
            jnp.dot(p_high, c_high, preferred_element_type=F32)
            + jnp.dot(p_low, c_high, preferred_element_type=F32)
            + jnp.dot(p_high, c_low, preferred_element_type=F32)
        )
        query = feature(x_ref[0, :, at], halo_ref[0, :, at], w_ref, 0, at)
        out_ref[:, at] = (query * (near_ref[:, at] + far)).astype(BF16)


def hyena_finish(near, streams, halo, short_weight, carried, rates, residues):
    rows, channels = near.shape
    edge = halo.shape[1]
    modes, groups = rates.shape
    filters = groups * LANES // channels
    terms = filters * modes
    wide = channels // STEPS
    by_block = lambda n: (0, n)
    lead = lambda n: (0, 0, n)
    whole = lambda n: (0, 0)
    return pl.pallas_call(
        functools.partial(hyena_out_body, filters),
        grid=(STEPS,),
        in_specs=[
            pl.BlockSpec((rows, wide), by_block),
            pl.BlockSpec((1, rows, wide), lead),
            pl.BlockSpec((1, edge, wide), lead),
            pl.BlockSpec((3, 3, wide), lead),
            pl.BlockSpec((modes, wide), by_block),
            pl.BlockSpec((modes, groups), whole),
            pl.BlockSpec((modes, groups), whole),
        ],
        out_specs=pl.BlockSpec((rows, wide), by_block),
        out_shape=jax.ShapeDtypeStruct((rows, channels), BF16),
        compiler_params=limits(16),
        cost_estimate=cost(6 * rows * terms * channels, 10 * rows * channels),
        name="hyena_finish",
    )(near, streams, halo, short_weight, carried, rates, residues)


def scan_states(ends, rate, rows):
    half = ends.shape[1] // 2
    index = lax.axis_index("ctx")
    count = lax.axis_size("ctx") // ROW
    core, side = index % 2, index // 2 % 2
    take = lambda matrix, which: lax.dynamic_slice_in_dim(matrix, which * half, half, 1)
    rate = take(rate, core)
    decay = lambda blocks: jnp.exp(-rate * float(rows * blocks))
    mine = take(ends, core)
    theirs = flip(take(ends, 1 - core), "ctx", 1)
    even = jnp.where(core == 0, mine, theirs)
    odd = jnp.where(core == 0, theirs, mine)
    chip = decay(1) * even + odd
    other = flip(chip, "ctx", 2)
    left = jnp.where(side == 0, chip, other)
    total = decay(2) * left + jnp.where(side == 0, other, chip)
    before = ahead(total, "ctx", ROW)
    reach = 2
    while reach < count:
        upto = total + decay(ROW) * before
        earlier = ahead(upto, "ctx", ROW * reach)
        before = before + decay(ROW * (reach - 1)) * earlier
        reach *= 2
    before = jnp.where(side == 0, before, decay(2) * before + left)
    second = decay(1) * before + even
    keep = jnp.where(core == 0, before, second)
    back = flip(jnp.where(core == 0, second, before), "ctx", 1)
    return jnp.concatenate(
        [jnp.where(core == 0, keep, back), jnp.where(core == 0, back, keep)], axis=1
    )


def lanes_from(start, size):
    return pl.ds(pl.multiple_of(start * size, size), size)


def front_body(attn, hyena, theirs_ref, edge_ref, sems):
    rows, half = theirs_ref.shape[1:]
    away = attn.at[:, :, lanes_from(1 - spot()[0], half)]
    edge = hyena.at[:, rows - EDGE : rows, :]
    copies = [
        pltpu.make_async_copy(away, theirs_ref, sems.at[0]),
        pltpu.make_async_copy(edge, edge_ref, sems.at[1]),
    ]
    for copy in copies:
        copy.start()
    for copy in copies:
        copy.wait()


def front(attn, hyena):
    count, rows, channels = attn.shape
    return pl.pallas_call(
        front_body,
        in_specs=[HBM, HBM],
        out_specs=[VMEM, VMEM],
        out_shape=[
            jax.ShapeDtypeStruct((count, rows, channels // 2), attn.dtype),
            jax.ShapeDtypeStruct((count, EDGE, channels), hyena.dtype),
        ],
        scratch_shapes=[pltpu.SemaphoreType.DMA((2,))],
        compiler_params=pltpu.CompilerParams(vmem_limit_bytes=ALL_VMEM - (18 << 17)),
        cost_estimate=cost(0, 4 * count * rows * channels // 2),
        name="front",
    )(attn, hyena)


def pack_body(first, streams_ref, theirs_ref, *outs):
    core, side, _, _ = spot()
    slots = (0, 1) if first == 0 else (1 - core, core)
    quarter = theirs_ref.shape[2] // 2
    for out, away in zip(outs, (0, 1)[-len(outs) :]):
        to = 1 - side if away else side
        for stream in range(first, 3):
            out[slots[0], stream - first] = streams_ref[stream, :, lanes_from(2 * core + to, quarter)]
            out[slots[1], stream - first] = theirs_ref[stream, :, lanes_from(to, quarter)]


def pack(streams, theirs, first, amount):
    _, rows, half = theirs.shape
    shape = jax.ShapeDtypeStruct((2, 3 - first, rows, half // 2), BF16)
    return pl.pallas_call(
        functools.partial(pack_body, first),
        in_specs=[VMEM, VMEM],
        out_specs=[VMEM] * amount,
        out_shape=[shape] * amount,
        compiler_params=limits(10),
        cost_estimate=cost(0, 8 * amount * rows * half),
        name="pack",
    )(streams, theirs)


def contig_start(docs_ref, position):
    first = jnp.zeros_like(position)
    bound = jnp.int32(0)
    for n in range(docs_ref.shape[0]):
        bound = bound + docs_ref[n]
        first = jnp.where(position >= bound, bound, first)
    return first


def row_part(streams, theirs, swap, slot, stream, quarter):
    core, side, _, _ = spot()
    if slot == 0:
        return streams.at[stream, :, lanes_from(2 * core + side, quarter)]
    if slot == 1:
        return theirs.at[stream, :, lanes_from(side, quarter)]
    return swap.at[slot - 2, stream]


SCALE = math.log2(math.e) / math.sqrt(HEAD)


KEYS = 256
GROUP = 2
CHUNK = 32


def attend_body(docs_ref, streams, theirs, swap, own, cross, acc_ref, m_ref, l_ref, q_s, k_s, v_s, bias_s, s_s, p_s, sems):
    _, side, place, row = spot()
    rows, quarter = q_s.shape[0] // ROW, q_s.shape[1]
    base = row * (ROW * rows)
    copies = []

    def bring(source, target):
        copies.append(pltpu.make_async_copy(source, target, sems.at[len(copies)]))
        copies[-1].start()

    for n in range(2):
        for old, which in ((own, side), (cross, 1 - side)):
            older = lanes_from(2 * which + 1 - n, rows)
            bring(old.at[n, 0], k_s.at[older])
            bring(old.at[n, 1], v_s.at[older])
    for slot in range(ROW):
        part = lambda stream: row_part(streams, theirs, swap, slot, stream, quarter)
        block = place ^ slot
        newer = lanes_from(ROW + block, rows)
        bring(part(0), q_s.at[lanes_from(block, rows)])
        bring(part(1), k_s.at[newer])
        bring(part(2), v_s.at[newer])
    for copy in copies:
        copy.wait()

    for group in range(ROW // GROUP):
        tall = GROUP * rows
        width = (ROW + GROUP * (group + 1)) * rows
        here = slice(group * tall, (group + 1) * tall)
        for block in range(GROUP):
            position = base + (group * GROUP + block) * rows + lax.broadcasted_iota(jnp.int32, (rows, 1), 0)
            first = contig_start(docs_ref, position)
            at = base - ROW * rows + lax.broadcasted_iota(jnp.int32, (rows, width), 1)
            bias_s[block * rows : (block + 1) * rows, 0:width] = jnp.where(
                (at >= first) & (at <= position), 0.0, -jnp.inf
            )
        for head in range(quarter // HEAD):
            lanes = slice(head * HEAD, (head + 1) * HEAD)
            turn = head % 2
            for n in range(0, width, KEYS):
                tile = slice(n, n + KEYS)
                s_s[turn, :, tile] = lax.dot_general(
                    q_s[here, lanes],
                    k_s[tile, lanes],
                    (((1,), (1,)), ((), ())),
                    preferred_element_type=F32,
                )
            for m in range(0, tall, CHUNK):
                some = slice(m, m + CHUNK)
                out = slice(group * tall + m, group * tall + m + CHUNK)
                top = None
                parts = []
                for n in range(0, width, LANES):
                    part = s_s[turn, some, n : n + LANES] + bias_s[some, n : n + LANES]
                    parts.append(part)
                    top = part if top is None else jnp.maximum(top, part)
                top = jnp.broadcast_to(jnp.max(top, axis=1, keepdims=True), (CHUNK, LANES))
                m_ref[out, lanes] = top
                below = jnp.zeros((CHUNK, LANES), F32)
                for n, part in enumerate(parts):
                    weight = jnp.exp2((part - top) * SCALE)
                    below = below + weight
                    p_s[turn, some, n * LANES : (n + 1) * LANES] = weight.astype(BF16)
                l_ref[out, lanes] = jnp.broadcast_to(jnp.sum(below, axis=1, keepdims=True), (CHUNK, LANES))
            acc_ref[here, lanes] = jnp.dot(
                p_s[turn, :, 0:width], v_s[0:width, lanes], preferred_element_type=F32
            )


def attend(doc_lengths, streams, theirs, swap, own, cross):
    _, _, rows, quarter = own.shape
    heads = quarter // HEAD
    return pl.pallas_call(
        attend_body,
        in_specs=[SMEM] + [ANY] * 5,
        out_specs=[VMEM] * 3,
        out_shape=[
            jax.ShapeDtypeStruct((ROW * rows, quarter), F32),
        ]
        * 3,
        scratch_shapes=[
            pltpu.VMEM((ROW * rows, quarter), BF16),
            pltpu.VMEM((2 * ROW * rows, quarter), BF16),
            pltpu.VMEM((2 * ROW * rows, quarter), BF16),
            pltpu.VMEM((GROUP * rows, 2 * ROW * rows), F32),
            pltpu.VMEM((2, GROUP * rows, 2 * ROW * rows), F32),
            pltpu.VMEM((2, GROUP * rows, 2 * ROW * rows), BF16),
            pltpu.SemaphoreType.DMA((5 * ROW,)),
        ],
        compiler_params=limits(20),
        cost_estimate=cost(26 * 4 * rows * rows * quarter, 14 * ROW * rows * quarter, 26 * heads * rows * rows),
        name="attend",
    )(doc_lengths, streams, theirs, swap, own, cross)


def attend_last_body(docs_ref, streams, theirs, swap, *refs):
    olds, (acc_ref, m_ref, l_ref), outs, (q_s, kv_s, o_s, sems) = refs[:4], refs[4:7], refs[7:11], refs[11:]
    _, side, place, row = spot()
    rows, quarter = q_s.shape[1:]
    base = row * (ROW * rows)
    copies = []

    def copy_of(source, target, n):
        return pltpu.make_async_copy(source, target, sems.at[n])

    for slot in range(ROW):
        copies.append(copy_of(row_part(streams, theirs, swap, slot, 0, quarter), q_s.at[place ^ slot], slot))
        copies[-1].start()
    for which in range(2):
        large, small = olds[2 * which : 2 * which + 2]
        arrived = [
            copy_of(small.at[0], kv_s.at[0], ROW),
            copy_of(large.at[1], kv_s.at[1], ROW + 1),
            copy_of(large.at[0], kv_s.at[2], ROW + 2),
        ]

        @pl.when(side == which)
        def _():
            for copy in arrived:
                copy.start()

    for copy in copies + arrived:
        copy.wait()
    heads = [slice(n, n + HEAD) for n in range(0, quarter, HEAD)]
    for block in range(ROW):
        slot = place ^ block
        here = slice(block * rows, (block + 1) * rows)
        seen = ROW - 1 - block
        width = seen * rows
        if not seen:
            for lanes in heads:
                o_s[slot, :, lanes] = (acc_ref[here, lanes] * (1.0 / l_ref[here, lanes])).astype(BF16)
            continue
        position = base + block * rows + lax.broadcasted_iota(jnp.int32, (rows, 1), 0)
        first = contig_start(docs_ref, position)
        at = base - (ROW + seen) * rows + lax.broadcasted_iota(jnp.int32, (rows, width), 1)
        allowed = at >= first
        scores = [
            lax.dot_general(
                q_s[block, :, lanes],
                kv_s[block : ROW - 1, 0, :, lanes].reshape(width, HEAD),
                (((1,), (1,)), ((), ())),
                preferred_element_type=F32,
            )
            for lanes in heads
        ]
        scores = [jnp.where(allowed, score, -jnp.inf) for score in scores]
        tops = [
            jnp.maximum(m_ref[here, lanes], jnp.max(score, axis=1, keepdims=True))
            for lanes, score in zip(heads, scores)
        ]
        weights = [
            jnp.exp2((score - jnp.concatenate([top] * seen, axis=1)) * SCALE)
            for score, top in zip(scores, tops)
        ]
        for lanes, top, weight in zip(heads, tops, weights):
            fade = jnp.exp2((m_ref[here, lanes] - top) * SCALE)
            share = 1.0 / (l_ref[here, lanes] * fade + jnp.sum(weight, axis=1, keepdims=True))
            more = jnp.dot(
                weight.astype(BF16),
                kv_s[block : ROW - 1, 1, :, lanes].reshape(width, HEAD),
                preferred_element_type=F32,
            )
            o_s[slot, :, lanes] = ((acc_ref[here, lanes] * fade + more) * share).astype(BF16)
    for slot, out in enumerate(outs):
        out[...] = o_s[slot]


def attend_last(doc_lengths, streams, theirs, swap, olds, acc, top, below):
    rows, quarter = acc.shape[0] // ROW, acc.shape[1]
    heads = quarter // HEAD
    return pl.pallas_call(
        attend_last_body,
        in_specs=[SMEM] + [ANY] * 7 + [VMEM] * 3,
        out_specs=[VMEM] * ROW,
        out_shape=[jax.ShapeDtypeStruct((rows, quarter), BF16)] * ROW,
        scratch_shapes=[
            pltpu.VMEM((ROW, rows, quarter), BF16),
            pltpu.VMEM((ROW - 1, 2, rows, quarter), BF16),
            pltpu.VMEM((ROW, rows, quarter), BF16),
            pltpu.SemaphoreType.DMA((2 * ROW,)),
        ],
        compiler_params=limits(16),
        cost_estimate=cost(6 * 4 * rows * rows * quarter, 12 * ROW * rows * quarter, 6 * heads * rows * rows),
        name="attend_last",
    )(doc_lengths, streams, theirs, swap, *olds, acc, top, below)


def assemble_body(*refs):
    place = spot()[2]
    *pieces, out_ref = refs
    quarter = pieces[0].shape[1]
    for slot, piece in enumerate(pieces):
        maker = place ^ slot
        which = 2 * (maker & 1) + lax.shift_right_logical(maker, 1)
        out_ref[:, lanes_from(which, quarter)] = piece[...]


def assemble(pieces):
    rows, quarter = pieces[0].shape
    return pl.pallas_call(
        assemble_body,
        in_specs=[VMEM] * ROW,
        out_specs=VMEM,
        out_shape=jax.ShapeDtypeStruct((rows, ROW * quarter), BF16),
        compiler_params=limits(6),
        cost_estimate=cost(0, 16 * rows * quarter),
        name="assemble",
    )(*pieces)


def on_device(hyena_qkv, short_weight, filter_rate, filter_residue, attn_qkv, doc_lengths):
    rows = attn_qkv.shape[0]
    inner = hyena_qkv.transpose(1, 0, 2)
    streams = attn_qkv.transpose(1, 0, 2)
    rates, residues = filter_rate.T, filter_residue.T
    theirs, edge = front(streams, inner)

    theirs = flip(theirs, "ctx", 1)
    edge = ahead(edge, "ctx", 1)
    own, cross = pack(streams, theirs, 1, 2)
    cross = ahead(cross, "ctx", ROW, 2)
    own = ahead(own, "ctx", ROW)
    (swap,) = pack(streams, theirs, 0, 1)
    swap = flip(swap, "ctx", 2)
    olds = (
        ahead(cross, "ctx", ROW, 0, ROW, 0),
        ahead(own[:1], "ctx", ROW, 0, ROW, 0),
        ahead(own, "ctx", ROW, 0, ROW, 1),
        ahead(cross[:1], "ctx", ROW, 0, ROW, 1),
    )

    mixed, ends, wide = hyena_ends(inner, edge, short_weight, rates)
    near = hyena_near(mixed, rates, residues)
    carried = scan_states(ends, wide, rows)
    hyena_out = hyena_finish(near, inner, edge, short_weight, carried, rates, residues)

    acc, top, below = attend(doc_lengths, streams, theirs, swap, own, cross)
    made = attend_last(doc_lengths, streams, theirs, swap, olds, acc, top, below)
    pieces = [made[0]] + [flip(made[n], "ctx", n) for n in range(1, ROW)]
    attn_out = assemble(pieces)
    return (hyena_out, attn_out)


def solution(mesh):
    in_specs = (
        P(("group", "ctx"), None, None),
        P(),
        P(),
        P(),
        P(("group", "ctx"), None, None),
        P("group"),
    )
    out_specs = (P(("group", "ctx"), None), P(("group", "ctx"), None))
    return jax.shard_map(on_device, mesh=mesh, in_specs=in_specs, out_specs=out_specs, check_vma=False)
```

profile of v0, /device:TPU:21, one launch (start us, length us, event | category | flops | bytes accessed | tf_op | source)
XLA Modules:
  0.0 85.1 jit_solution(5528523435031529008)
XLA Ops:
  0.7 2.2 %front.1 = (bf16[3,128,1024]{2,1,0:T(8,128)(2,1)}, bf16[3,8,2048]{2,1,0:T(8,128)(2,1)}) custom-call(bf16[3,128,2048]{2,1,0:T(8,128)(2,1)} %bitcast.4, bf16[3,128,2048]{2,1,0:T(8,128)(2,1)} %bitcast.9), custom_call_target="tpu_custom_call" | custom-call | bytes 1572864 | tf_op jit(solution)/shard_map/front/pallas_call | solution.py:332
  2.9 0.7 collective-permute-start.6
  3.6 3.2 %collective-permute-start = (bf16[3,8,2048]{2,1,0:T(8,128)(2,1)}, bf16[3,8,2048]{2,1,0:T(8,128)(2,1)S(1)}, u32[]{:S(2)}, u32[]{:S(2)}) collective-permute-start(bf16[3,8,2048]{2,1,0:T(8,128)(2,1)} %get-tuple-element.16), channel_id=1, source_target_pairs={{0,1},{1,2},{2,3},{3,4},{4,5},{5,6},{6,7},{7,8},{8,9},{9,10},{10,1... | collective-permute-start | bytes 294920 | tf_op jit(solution)/shard_map/ppermute | solution.py:37
  6.8 1.9 %collective-permute-done.halo_ref = bf16[3,8,2048]{2,1,0:T(8,128)(2,1)S(1)} collective-permute-done((bf16[3,8,2048]{2,1,0:T(8,128)(2,1)}, bf16[3,8,2048]{2,1,0:T(8,128)(2,1)S(1)}, u32[]{:S(2)}, u32[]{:S(2)}) %collective-permute-start) | collective-permute-done | bytes 98336 | tf_op jit(solution)/shard_map/ppermute | solution.py:37
  8.8 2.9 %hyena_ends.1 = (bf16[128,2048]{1,0:T(8,128)(2,1)S(1)}, f32[16,2048]{1,0:T(8,128)}, f32[16,2048]{1,0:T(8,128)S(1)}) custom-call(bf16[3,128,2048]{2,1,0:T(8,128)(2,1)S(1)} %bitcast.10, bf16[3,8,2048]{2,1,0:T(8,128)(2,1)S(1)} %collective-permute-done.halo_ref, f32[3,3,2048]{2,1,0:T(4,128)S(1)} %copy-done.2, f32[16,128]{1,0:T(8,128)S(1)} %bitcast.12), custom_call_target="tpu_custom_call" | custom-call | flops 134217728 | bytes 2097152 | tf_op jit(solution)/shard_map/hyena_ends/pallas_call | solution.py:138
  11.6 0.8 copy-done.6
  12.4 0.8 constant_dynamic-slice_fusion
  13.3 1.2 %collective-permute-start.1 = (f32[16,1024]{1,0:T(8,128)S(1)}, f32[16,1024]{1,0:T(8,128)}, u32[]{:S(2)}, u32[]{:S(2)}) collective-permute-start(f32[16,1024]{1,0:T(8,128)S(1)} %constant_dynamic-slice_fusion), channel_id=1, source_target_pairs={{0,1},{1,0},{2,3},{3,2},{4,5},{5,4},{6,7},{7,6},{8,9},{9,8},{10,11... | collective-permute-start | bytes 196616 | tf_op jit(solution)/shard_map/ppermute | solution.py:23
  14.5 1.0 %collective-permute-done.1 = f32[16,1024]{1,0:T(8,128)} collective-permute-done((f32[16,1024]{1,0:T(8,128)S(1)}, f32[16,1024]{1,0:T(8,128)}, u32[]{:S(2)}, u32[]{:S(2)}) %collective-permute-start.1) | collective-permute-done | bytes 65568 | tf_op jit(solution)/shard_map/ppermute | solution.py:23
  15.5 0.9 %select_add_fusion.1 = f32[16,1024]{1,0:T(8,128)S(1)} fusion(f32[16,1024]{1,0:T(8,128)} %collective-permute-done.1, f32[16,2048]{1,0:T(8,128)} %get-tuple-element.19, s32[]{:T(128)S(6)} %select_n.69, f32[16,2048]{1,0:T(8,128)S(1)} %get-tuple-element.18, pred[]{:T(512)S(6)} %eq.7), kind=kLoop, calls=%fused_computation.6 | loop fusion | flops 98304 | bytes 262149 | tf_op jit(solution)/shard_map/add | solution.py:292
  16.4 1.2 %collective-permute-start.2 = (f32[16,1024]{1,0:T(8,128)S(1)}, f32[16,1024]{1,0:T(8,128)}, u32[]{:S(2)}, u32[]{:S(2)}) collective-permute-start(f32[16,1024]{1,0:T(8,128)S(1)} %select_add_fusion.1), channel_id=1, source_target_pairs={{0,2},{1,3},{2,0},{3,1},{4,6},{5,7},{6,4},{7,5},{8,10},{9,11},{10,... | collective-permute-start | bytes 196616 | tf_op jit(solution)/shard_map/ppermute | solution.py:23
  17.6 1.2 %pack.3 = (bf16[2,2,128,512]{3,2,1,0:T(8,128)(2,1)S(1)}, bf16[2,2,128,512]{3,2,1,0:T(8,128)(2,1)S(1)}) custom-call(bf16[3,128,2048]{2,1,0:T(8,128)(2,1)S(1)} %bitcast.5, bf16[3,128,1024]{2,1,0:T(8,128)(2,1)} %collective-permute-done.6.theirs_ref.theirs), custom_call_target="tpu_custom_call" | custom-call | bytes 2097152 | tf_op jit(solution)/shard_map/pack/pallas_call | solution.py:361
  18.8 3.2 %collective-permute-start.10 = (bf16[2,2,128,512]{3,2,1,0:T(8,128)(2,1)S(1)}, bf16[2,2,128,512]{3,2,1,0:T(8,128)(2,1)S(1)}, u32[]{:S(2)}, u32[]{:S(2)}) collective-permute-start(bf16[2,2,128,512]{3,2,1,0:T(8,128)(2,1)S(1)} %get-tuple-element.22), channel_id=1, source_target_pairs={{0,4},{1,5},{2,6},{3,7},{4,8},{5,9},{6,10},{7,11},{8,12},{9,13},{1... | collective-permute-start | bytes 1572872 | tf_op jit(solution)/shard_map/ppermute | solution.py:37
  22.0 1.9 %collective-permute-start.8 = (bf16[2,2,128,512]{3,2,1,0:T(8,128)(2,1)S(1)}, bf16[2,2,128,512]{3,2,1,0:T(8,128)(2,1)S(1)}, u32[]{:S(2)}, u32[]{:S(2)}) collective-permute-start(bf16[2,2,128,512]{3,2,1,0:T(8,128)(2,1)S(1)} %get-tuple-element.21), channel_id=1, source_target_pairs={{0,6},{1,7},{2,4},{3,5},{4,10},{5,11},{6,8},{7,9},{8,14},{9,15},{1... | collective-permute-start | bytes 1572872 | tf_op jit(solution)/shard_map/ppermute | solution.py:37
  24.0 0.9 %select_add_fusion = f32[16,1024]{1,0:T(8,128)S(1)} fusion(f32[16,1024]{1,0:T(8,128)} %collective-permute-done.2, f32[16,1024]{1,0:T(8,128)S(1)} %select_add_fusion.1, f32[16,2048]{1,0:T(8,128)S(1)} %get-tuple-element.18, s32[]{:T(128)S(6)} %select_n.69, pred[]{:T(512)S(6)} %eq.8), kind=kLoop, calls=%fused_computation.5 | loop fusion | flops 98304 | bytes 262149 | tf_op jit(solution)/shard_map/add | solution.py:295
  24.9 2.1 %collective-permute-start.3 = (f32[16,1024]{1,0:T(8,128)S(1)}, f32[16,1024]{1,0:T(8,128)S(1)}, u32[]{:S(2)}, u32[]{:S(2)}) collective-permute-start(f32[16,1024]{1,0:T(8,128)S(1)} %select_add_fusion), channel_id=1, source_target_pairs={{0,4},{1,5},{2,6},{3,7},{4,8},{5,9},{6,10},{7,11},{8,12},{9,13},{1... | collective-permute-start | bytes 196616 | tf_op jit(solution)/shard_map/ppermute | solution.py:37
  26.9 1.2 %pack.2 = bf16[2,3,128,512]{3,2,1,0:T(8,128)(2,1)S(1)} custom-call(bf16[3,128,2048]{2,1,0:T(8,128)(2,1)S(1)} %bitcast.6, bf16[3,128,1024]{2,1,0:T(8,128)(2,1)} %collective-permute-done.6.theirs_ref.theirs), custom_call_target="tpu_custom_call" | custom-call | bytes 1048576 | tf_op jit(solution)/shard_map/pack/pallas_call | solution.py:361
  28.7 17.5 %collective-permute-done.3 = f32[16,1024]{1,0:T(8,128)S(1)} collective-permute-done((f32[16,1024]{1,0:T(8,128)S(1)}, f32[16,1024]{1,0:T(8,128)S(1)}, u32[]{:S(2)}, u32[]{:S(2)}) %collective-permute-start.3) | collective-permute-done | bytes 65568 | tf_op jit(solution)/shard_map/ppermute | solution.py:37
  46.3 1.3 %collective-permute-start.4 = (f32[16,1024]{1,0:T(8,128)S(1)}, f32[16,1024]{1,0:T(8,128)S(1)}, u32[]{:S(2)}, u32[]{:S(2)}) collective-permute-start(f32[16,1024]{1,0:T(8,128)S(1)} %multiply_add_fusion.1), channel_id=1, source_target_pairs={{0,8},{1,9},{2,10},{3,11},{4,12},{5,13},{6,14},{7,15},{16,24},{17,... | collective-permute-start | bytes 196616 | tf_op jit(solution)/shard_map/ppermute | solution.py:37
  47.6 3.2 %collective-permute-start.12 = (bf16[2,2,128,512]{3,2,1,0:T(8,128)(2,1)S(1)}, bf16[2,2,128,512]{3,2,1,0:T(8,128)(2,1)S(1)}, u32[]{:S(2)}, u32[]{:S(2)}) collective-permute-start(bf16[2,2,128,512]{3,2,1,0:T(8,128)(2,1)S(1)} %collective-permute-done.10.own), channel_id=1, source_target_pairs={{6,10},{7,11},{10,14},{11,15},{22,26},{23,27},{26,30},{27,31}} | collective-permute-start | bytes 1572872 | tf_op jit(solution)/shard_map/ppermute | solution.py:37
  50.8 0.7 collective-permute-start.9
  51.5 0.7 collective-permute-done.4
  52.2 1.0 %broadcast_select_fusion.3 = (f32[16,1024]{1,0:T(8,128)S(1)}, f32[16,1024]{1,0:T(8,128)S(1)}, f32[16,1024]{1,0:T(8,128)S(1)}) fusion(pred[]{:T(512)S(6)} %eq.7, f32[16,1024]{1,0:T(8,128)} %collective-permute-done.1, f32[16,2048]{1,0:T(8,128)} %get-tuple-element.19, s32[]{:T(128)S(6)} %select_n.69, f32[16,2048]{1,0:T(8,128)S(1)} %get-tuple-element.18, ...), kind=kLoop, calls=%fused_computation.14 | loop fusion | flops 229376 | bytes 655366 | tf_op jit(solution)/shard_map/jit(_where)/select_n | solution.py:306
  53.2 2.7 %collective-permute-start.5 = (f32[16,1024]{1,0:T(8,128)S(1)}, f32[16,1024]{1,0:T(8,128)S(1)}, u32[]{:S(2)}, u32[]{:S(2)}) collective-permute-start(f32[16,1024]{1,0:T(8,128)S(1)} %get-tuple-element.30), channel_id=1, source_target_pairs={{0,1},{1,0},{2,3},{3,2},{4,5},{5,4},{6,7},{7,6},{8,9},{9,8},{10,11... | collective-permute-start | bytes 196616 | tf_op jit(solution)/shard_map/ppermute | solution.py:23
  55.9 4.3 %hyena_near.1.near_ref = f32[128,2048]{1,0:T(8,128)S(1)} custom-call(bf16[128,2048]{1,0:T(8,128)(2,1)S(1)} %copy-done.7, f32[16,128]{1,0:T(8,128)S(1)} %bitcast.13, f32[16,128]{1,0:T(8,128)S(1)} %bitcast.15), custom_call_target="tpu_custom_call" | custom-call | flops 536870912 | bytes 3145728 | tf_op jit(solution)/shard_map/hyena_near/pallas_call | solution.py:201
  61.0 4.5 %collective-permute-start.13 = (bf16[1,2,128,512]{3,2,1,0:T(8,128)(2,1)S(1)}, bf16[1,2,128,512]{3,2,1,0:T(8,128)(2,1)S(1)}, u32[]{:S(2)}, u32[]{:S(2)}) collective-permute-start(bf16[1,2,128,512]{3,2,1,0:T(8,128)(2,1)S(1)} %slice.9), channel_id=1, source_target_pairs={{6,10},{7,11},{10,14},{11,15},{22,26},{23,27},{26,30},{27,31}} | collective-permute-start | bytes 786440 | tf_op jit(solution)/shard_map/ppermute | solution.py:37
  65.6 7.3 %attend.1 = (f32[512,512]{1,0:T(8,128)S(1)}, f32[512,512]{1,0:T(8,128)S(1)}, f32[512,512]{1,0:T(8,128)S(1)}) custom-call(s32[4]{0:T(128)S(1)} %copy-done.5, bf16[3,128,2048]{2,1,0:T(8,128)(2,1)S(1)} %bitcast.7, bf16[3,128,1024]{2,1,0:T(8,128)(2,1)} %collective-permute-done.6.theirs_ref.theirs, bf16[2,3,128,512]{3,2,1,0:T(8,128)(2,1)S(1)} %collective-permute-done.7.swap, ...), custom_call_target="tpu_custom_call" | custom-call | flops 872415232 | bytes 3670016 | tf_op jit(solution)/shard_map/attend/pallas_call | solution.py:470
  72.9 2.9 %attend_last.1 = (bf16[128,512]{1,0:T(8,128)(2,1)S(1)}, bf16[128,512]{1,0:T(8,128)(2,1)S(1)}, bf16[128,512]{1,0:T(8,128)(2,1)S(1)}, bf16[128,512]{1,0:T(8,128)(2,1)S(1)}) custom-call(s32[4]{0:T(128)S(1)} %copy-done.5, bf16[3,128,2048]{2,1,0:T(8,128)(2,1)S(1)} %bitcast.8, bf16[3,128,1024]{2,1,0:T(8,128)(2,1)} %collective-permute-done.6.theirs_ref.theirs, ...), custom_call_target="tpu_custom_call" | custom-call | flops 201326592 | bytes 3145728 | tf_op jit(solution)/shard_map/attend_last/pallas_call | solution.py:569
  76.4 1.6 %collective-permute-start.16 = (bf16[128,512]{1,0:T(8,128)(2,1)S(1)}, bf16[128,512]{1,0:T(8,128)(2,1)S(1)}, u32[]{:S(2)}, u32[]{:S(2)}) collective-permute-start(bf16[128,512]{1,0:T(8,128)(2,1)S(1)} %get-tuple-element.29), channel_id=1, source_target_pairs={{0,3},{1,2},{2,1},{3,0},{4,7},{5,6},{6,5},{7,4},{8,11},{9,10},{10,... | collective-permute-start | bytes 393224 | tf_op jit(solution)/shard_map/ppermute | solution.py:23
  78.1 3.4 %hyena_finish.1 = bf16[128,2048]{1,0:T(8,128)(2,1)} custom-call(f32[128,2048]{1,0:T(8,128)S(1)} %hyena_near.1.near_ref, bf16[3,128,2048]{2,1,0:T(8,128)(2,1)S(1)} %bitcast.11, bf16[3,8,2048]{2,1,0:T(8,128)(2,1)S(1)} %collective-permute-done.halo_ref, f32[3,3,2048]{2,1,0:T(4,128)S(1)} %copy-done.2, f32[16,2048]{1,0:T(8,128)S(1)} %pad_maximum_fusion.carried_ref, ...), custom_call_target="tpu_custom_call" | custom-call | flops 201326592 | bytes 2621440 | tf_op jit(solution)/shard_map/hyena_finish/pallas_call | solution.py:260
  81.5 2.8 %collective-permute-done.16.refs_3_ = bf16[128,512]{1,0:T(8,128)(2,1)S(1)} collective-permute-done((bf16[128,512]{1,0:T(8,128)(2,1)S(1)}, bf16[128,512]{1,0:T(8,128)(2,1)S(1)}, u32[]{:S(2)}, u32[]{:S(2)}) %collective-permute-start.16) | collective-permute-done | bytes 131104 | tf_op jit(solution)/shard_map/ppermute | solution.py:23
  84.3 0.8 assemble.1
  (36 shorter events, 2.0 us)
Async XLA Ops:
  0.6 8.1 %copy-start.1 = (bf16[128,3,2048]{2,0,1:T(8,128)(2,1)S(1)}, bf16[128,3,2048]{2,0,1:T(8,128)(2,1)}, u32[]{:S(2)}) copy-start(bf16[128,3,2048]{2,0,1:T(8,128)(2,1)} %param.6) | copy-start | bytes 4718596
  0.6 8.1 %copy-start.2 = (f32[3,3,2048]{2,1,0:T(4,128)S(1)}, f32[3,3,2048]{2,1,0:T(4,128)}, u32[]{:S(2)}) copy-start(f32[3,3,2048]{2,1,0:T(4,128)} %w_ref.3) | copy-start | bytes 221188
  0.6 8.1 %copy-start.3 = (f32[128,16]{0,1:T(8,128)S(1)}, f32[128,16]{0,1:T(8,128)}, u32[]{:S(2)}) copy-start(f32[128,16]{0,1:T(8,128)} %param.8) | copy-start | bytes 24580
  2.9 14.7 %copy-start = (bf16[128,3,2048]{2,0,1:T(8,128)(2,1)S(1)}, bf16[128,3,2048]{2,0,1:T(8,128)(2,1)}, u32[]{:S(2)}) copy-start(bf16[128,3,2048]{2,0,1:T(8,128)(2,1)} %param.10) | copy-start | bytes 4718596
  2.9 14.7 %collective-permute-start.6 = (bf16[3,128,1024]{2,1,0:T(8,128)(2,1)}, bf16[3,128,1024]{2,1,0:T(8,128)(2,1)}, u32[]{:S(2)}, u32[]{:S(2)}) collective-permute-start(bf16[3,128,1024]{2,1,0:T(8,128)(2,1)} %get-tuple-element.20), channel_id=1, source_target_pairs={{0,1},{1,0},{2,3},{3,2},{4,5},{5,4},{6,7},{7,6},{8,9},{9,8},{10,11... | collective-permute-start | bytes 2359304 | tf_op jit(solution)/shard_map/ppermute | solution.py:23
  3.6 5.1 %collective-permute-start = (bf16[3,8,2048]{2,1,0:T(8,128)(2,1)}, bf16[3,8,2048]{2,1,0:T(8,128)(2,1)S(1)}, u32[]{:S(2)}, u32[]{:S(2)}) collective-permute-start(bf16[3,8,2048]{2,1,0:T(8,128)(2,1)} %get-tuple-element.16), channel_id=1, source_target_pairs={{0,1},{1,2},{2,3},{3,4},{4,5},{5,6},{6,7},{7,8},{8,9},{9,10},{10,1... | collective-permute-start | bytes 294920 | tf_op jit(solution)/shard_map/ppermute | solution.py:37
  11.6 0.8 copy-start.6
  13.3 2.2 %collective-permute-start.1 = (f32[16,1024]{1,0:T(8,128)S(1)}, f32[16,1024]{1,0:T(8,128)}, u32[]{:S(2)}, u32[]{:S(2)}) collective-permute-start(f32[16,1024]{1,0:T(8,128)S(1)} %constant_dynamic-slice_fusion), channel_id=1, source_target_pairs={{0,1},{1,0},{2,3},{3,2},{4,5},{5,4},{6,7},{7,6},{8,9},{9,8},{10,11... | collective-permute-start | bytes 196616 | tf_op jit(solution)/shard_map/ppermute | solution.py:23
  16.4 7.6 %collective-permute-start.2 = (f32[16,1024]{1,0:T(8,128)S(1)}, f32[16,1024]{1,0:T(8,128)}, u32[]{:S(2)}, u32[]{:S(2)}) collective-permute-start(f32[16,1024]{1,0:T(8,128)S(1)} %select_add_fusion.1), channel_id=1, source_target_pairs={{0,2},{1,3},{2,0},{3,1},{4,6},{5,7},{6,4},{7,5},{8,10},{9,11},{10,... | collective-permute-start | bytes 196616 | tf_op jit(solution)/shard_map/ppermute | solution.py:23
  18.8 28.8 %collective-permute-start.10 = (bf16[2,2,128,512]{3,2,1,0:T(8,128)(2,1)S(1)}, bf16[2,2,128,512]{3,2,1,0:T(8,128)(2,1)S(1)}, u32[]{:S(2)}, u32[]{:S(2)}) collective-permute-start(bf16[2,2,128,512]{3,2,1,0:T(8,128)(2,1)S(1)} %get-tuple-element.22), channel_id=1, source_target_pairs={{0,4},{1,5},{2,6},{3,7},{4,8},{5,9},{6,10},{7,11},{8,12},{9,13},{1... | collective-permute-start | bytes 1572872 | tf_op jit(solution)/shard_map/ppermute | solution.py:37
  22.0 28.8 %collective-permute-start.8 = (bf16[2,2,128,512]{3,2,1,0:T(8,128)(2,1)S(1)}, bf16[2,2,128,512]{3,2,1,0:T(8,128)(2,1)S(1)}, u32[]{:S(2)}, u32[]{:S(2)}) collective-permute-start(bf16[2,2,128,512]{3,2,1,0:T(8,128)(2,1)S(1)} %get-tuple-element.21), channel_id=1, source_target_pairs={{0,6},{1,7},{2,4},{3,5},{4,10},{5,11},{6,8},{7,9},{8,14},{9,15},{1... | collective-permute-start | bytes 1572872 | tf_op jit(solution)/shard_map/ppermute | solution.py:37
  24.8 31.1 %copy-start.4 = (f32[128,16]{0,1:T(8,128)S(1)}, f32[128,16]{0,1:T(8,128)}, u32[]{:S(2)}) copy-start(f32[128,16]{0,1:T(8,128)} %param.9) | copy-start | bytes 24580
  24.8 31.1 %copy-start.7 = (bf16[128,2048]{1,0:T(8,128)(2,1)S(1)}, bf16[128,2048]{1,0:T(8,128)(2,1)}, u32[]{:S(2)}) copy-start(bf16[128,2048]{1,0:T(8,128)(2,1)} %copy-done.6) | copy-start | bytes 1572868
  24.9 21.4 %collective-permute-start.3 = (f32[16,1024]{1,0:T(8,128)S(1)}, f32[16,1024]{1,0:T(8,128)S(1)}, u32[]{:S(2)}, u32[]{:S(2)}) collective-permute-start(f32[16,1024]{1,0:T(8,128)S(1)} %select_add_fusion), channel_id=1, source_target_pairs={{0,4},{1,5},{2,6},{3,7},{4,8},{5,9},{6,10},{7,11},{8,12},{9,13},{1... | collective-permute-start | bytes 196616 | tf_op jit(solution)/shard_map/ppermute | solution.py:37
  28.1 37.4 %collective-permute-start.7 = (bf16[2,3,128,512]{3,2,1,0:T(8,128)(2,1)S(1)}, bf16[2,3,128,512]{3,2,1,0:T(8,128)(2,1)S(1)}, u32[]{:S(2)}, u32[]{:S(2)}) collective-permute-start(bf16[2,3,128,512]{3,2,1,0:T(8,128)(2,1)S(1)} %pack.2), channel_id=1, source_target_pairs={{0,2},{1,3},{2,0},{3,1},{4,6},{5,7},{6,4},{7,5},{8,10},{9,11},{10,... | collective-permute-start | bytes 2359304 | tf_op jit(solution)/shard_map/ppermute | solution.py:23
  46.3 6.0 %collective-permute-start.4 = (f32[16,1024]{1,0:T(8,128)S(1)}, f32[16,1024]{1,0:T(8,128)S(1)}, u32[]{:S(2)}, u32[]{:S(2)}) collective-permute-start(f32[16,1024]{1,0:T(8,128)S(1)} %multiply_add_fusion.1), channel_id=1, source_target_pairs={{0,8},{1,9},{2,10},{3,11},{4,12},{5,13},{6,14},{7,15},{16,24},{17,... | collective-permute-start | bytes 196616 | tf_op jit(solution)/shard_map/ppermute | solution.py:37
  47.6 25.4 %collective-permute-start.12 = (bf16[2,2,128,512]{3,2,1,0:T(8,128)(2,1)S(1)}, bf16[2,2,128,512]{3,2,1,0:T(8,128)(2,1)S(1)}, u32[]{:S(2)}, u32[]{:S(2)}) collective-permute-start(bf16[2,2,128,512]{3,2,1,0:T(8,128)(2,1)S(1)} %collective-permute-done.10.own), channel_id=1, source_target_pairs={{6,10},{7,11},{10,14},{11,15},{22,26},{23,27},{26,30},{27,31}} | collective-permute-start | bytes 1572872 | tf_op jit(solution)/shard_map/ppermute | solution.py:37
  50.8 22.2 %collective-permute-start.9 = (bf16[2,2,128,512]{3,2,1,0:T(8,128)(2,1)S(1)}, bf16[2,2,128,512]{3,2,1,0:T(8,128)(2,1)S(1)}, u32[]{:S(2)}, u32[]{:S(2)}) collective-permute-start(bf16[2,2,128,512]{3,2,1,0:T(8,128)(2,1)S(1)} %collective-permute-done.8.cross), channel_id=1, source_target_pairs={{4,8},{5,9},{8,12},{9,13},{20,24},{21,25},{24,28},{25,29}} | collective-permute-start | bytes 1572872 | tf_op jit(solution)/shard_map/ppermute | solution.py:37
  53.2 7.8 %collective-permute-start.5 = (f32[16,1024]{1,0:T(8,128)S(1)}, f32[16,1024]{1,0:T(8,128)S(1)}, u32[]{:S(2)}, u32[]{:S(2)}) collective-permute-start(f32[16,1024]{1,0:T(8,128)S(1)} %get-tuple-element.30), channel_id=1, source_target_pairs={{0,1},{1,0},{2,3},{3,2},{4,5},{5,4},{6,7},{7,6},{8,9},{9,8},{10,11... | collective-permute-start | bytes 196616 | tf_op jit(solution)/shard_map/ppermute | solution.py:23
  55.9 9.6 %copy-start.5 = (s32[4]{0:T(128)S(1)}, s32[4]{0:T(128)}, u32[]{:S(2)}) copy-start(s32[4]{0:T(128)} %docs_ref.3) | copy-start | bytes 52
  60.3 12.6 %collective-permute-start.11 = (bf16[1,2,128,512]{3,2,1,0:T(8,128)(2,1)S(1)}, bf16[1,2,128,512]{3,2,1,0:T(8,128)(2,1)S(1)}, u32[]{:S(2)}, u32[]{:S(2)}) collective-permute-start(bf16[1,2,128,512]{3,2,1,0:T(8,128)(2,1)S(1)} %slice.8), channel_id=1, source_target_pairs={{4,8},{5,9},{8,12},{9,13},{20,24},{21,25},{24,28},{25,29}} | collective-permute-start | bytes 786440 | tf_op jit(solution)/shard_map/ppermute | solution.py:37
  61.0 11.9 %collective-permute-start.13 = (bf16[1,2,128,512]{3,2,1,0:T(8,128)(2,1)S(1)}, bf16[1,2,128,512]{3,2,1,0:T(8,128)(2,1)S(1)}, u32[]{:S(2)}, u32[]{:S(2)}) collective-permute-start(bf16[1,2,128,512]{3,2,1,0:T(8,128)(2,1)S(1)} %slice.9), channel_id=1, source_target_pairs={{6,10},{7,11},{10,14},{11,15},{22,26},{23,27},{26,30},{27,31}} | collective-permute-start | bytes 786440 | tf_op jit(solution)/shard_map/ppermute | solution.py:37
  75.8 5.6 %collective-permute-start.14 = (bf16[128,512]{1,0:T(8,128)(2,1)S(1)}, bf16[128,512]{1,0:T(8,128)(2,1)S(1)}, u32[]{:S(2)}, u32[]{:S(2)}) collective-permute-start(bf16[128,512]{1,0:T(8,128)(2,1)S(1)} %get-tuple-element.27), channel_id=1, source_target_pairs={{0,1},{1,0},{2,3},{3,2},{4,5},{5,4},{6,7},{7,6},{8,9},{9,8},{10,11... | collective-permute-start | bytes 393224 | tf_op jit(solution)/shard_map/ppermute | solution.py:23
  76.2 5.3 %collective-permute-start.15 = (bf16[128,512]{1,0:T(8,128)(2,1)S(1)}, bf16[128,512]{1,0:T(8,128)(2,1)S(1)}, u32[]{:S(2)}, u32[]{:S(2)}) collective-permute-start(bf16[128,512]{1,0:T(8,128)(2,1)S(1)} %get-tuple-element.28), channel_id=1, source_target_pairs={{0,2},{1,3},{2,0},{3,1},{4,6},{5,7},{6,4},{7,5},{8,10},{9,11},{10,... | collective-permute-start | bytes 393224 | tf_op jit(solution)/shard_map/ppermute | solution.py:23
  76.4 7.8 %collective-permute-start.16 = (bf16[128,512]{1,0:T(8,128)(2,1)S(1)}, bf16[128,512]{1,0:T(8,128)(2,1)S(1)}, u32[]{:S(2)}, u32[]{:S(2)}) collective-permute-start(bf16[128,512]{1,0:T(8,128)(2,1)S(1)} %get-tuple-element.29), channel_id=1, source_target_pairs={{0,3},{1,2},{2,1},{3,0},{4,7},{5,6},{6,5},{7,4},{8,11},{9,10},{10,... | collective-permute-start | bytes 393224 | tf_op jit(solution)/shard_map/ppermute | solution.py:23
where the time goes:
time: 85.7 us; the launch traced here: 85.1 us
  starting transfers between devices  29.4 us (34%)
  Pallas kernels  26.3 us (31%)
  waiting for transfers between devices  24 us (28%)
  other arithmetic  2.78 us (3%)
  local copies, waits for them, and re-layouts  1.71 us (2%)
  between operations  0.94 us (1%)
    ppermute x9, starting transfers between devices, ahead(): return lax.ppermute(value, axis, pairs)  20.7 us
    ppermute x9, waiting for transfers between devices, ahead(): return lax.ppermute(value, axis, pairs)  20.2 us
    ppermute x8, starting transfers between devices, flip(): return lax.ppermute(value, axis, [(at, at ^ bit) for at in range(count)])  8.65 us
    pallas_call x1, Pallas kernels, attend(): pl.pallas_call(attend_body, in_specs=[SMEM] + [ANY] * 5, out_specs=[VMEM]...  7.34 us
    pallas_call x1, Pallas kernels, hyena_near(): pl.pallas_call(functools.partial(hyena_near_body, filters), grid=(STEPS,)...  4.34 us
    ppermute x8, waiting for transfers between devices, flip(): return lax.ppermute(value, axis, [(at, at ^ bit) for at in range(count)])  3.82 us
    pallas_call x1, Pallas kernels, hyena_finish(): pl.pallas_call(functools.partial(hyena_out_body, filters), grid=(STEPS,),...  3.42 us
    pallas_call x1, Pallas kernels, attend_last(): pl.pallas_call(attend_last_body, in_specs=[SMEM] + [ANY] * 7 + [VMEM] * 3...  2.89 us
  transfers between devices with their start and end apart: 17, of which 5 were waited for; matrix products, arithmetic and copies ran while one was open for 4% of the time, Pallas kernels for 24%

commit v1 on v0

--- a/solution.py
+++ b/solution.py
@@ -96,7 +96,9 @@
     return jnp.concatenate([jnp.broadcast_to(c, (c.shape[0], lanes)) for c in columns], axis=0)
 
 
-def hyena_ends_body(filters, x_ref, halo_ref, w_ref, rate_ref, mixed_ref, ends_ref, wide_ref):
+def hyena_ends_body(
+    filters, x_ref, halo_ref, w_ref, rate_ref, res_ref, mixed_ref, keep_ref, away_ref, wide_ref, gain_ref
+):
     rows = x_ref.shape[1]
     modes, groups = rate_ref.shape
     parts = groups // STEPS // filters
@@ -104,11 +106,15 @@
     lanes = x_ref.shape[2] // parts
     width = lanes // filters
     rates = of_step(rate_ref)
+    coeffs = of_step(res_ref) * jnp.sqrt(2.0 * rates / modes)
     lag = (rows - 1 - lax.broadcasted_iota(jnp.int32, (terms, rows), 1)).astype(F32)
     own = same_filter(modes, width, terms, lanes)
     pick = lambda matrix: jnp.sum(jnp.where(own, matrix, 0.0).reshape(filters, modes, lanes), axis=0)
+    step = pl.program_id(0)
+    mine = step // (STEPS // 2) == spot()[0]
     for part in range(parts):
         at = slice(part * lanes, (part + 1) * lanes)
+        there = pl.ds(pl.multiple_of((step % (STEPS // 2)) * (parts * lanes) + part * lanes, lanes), lanes)
         key, value = (feature(x_ref[n, :, at], halo_ref[n, :, at], w_ref, n, at) for n in (1, 2))
         mixed = (key * value).astype(BF16)
         mixed_ref[:, at] = mixed
@@ -116,25 +122,35 @@
         powers = jnp.exp(-rate * lag)
         high = powers.astype(BF16)
         low = (powers - high.astype(F32)).astype(BF16)
-        ends = jnp.dot(high, mixed, preferred_element_type=F32) + jnp.dot(
-            low, mixed, preferred_element_type=F32
+        ends = pick(
+            jnp.dot(high, mixed, preferred_element_type=F32)
+            + jnp.dot(low, mixed, preferred_element_type=F32)
         )
-        ends_ref[:, at] = pick(ends)
-        wide_ref[:, at] = pick(rate)
+
+        @pl.when(mine)
+        def _():
+            keep_ref[:, there] = ends
+            wide_ref[:, there] = pick(rate)
+            gain_ref[:, there] = pick(down(coeffs, part, filters, rows))
+
+        @pl.when(jnp.logical_not(mine))
+        def _():
+            away_ref[:, there] = ends
 
 
 STEPS = 4
 
 
-def hyena_ends(streams, halo, short_weight, rates):
+def hyena_ends(streams, halo, short_weight, rates, residues):
     _, rows, channels = streams.shape
     edge = halo.shape[1]
     modes, groups = rates.shape
     filters = groups * LANES // channels
     terms = filters * modes
     wide = channels // STEPS
-    by_block = lambda n: (0, n)
     lead = lambda n: (0, 0, n)
+    whole = lambda n: (0, 0)
+    half = (modes, channels // 2)
     return pl.pallas_call(
         functools.partial(hyena_ends_body, filters),
         grid=(STEPS,),
@@ -142,22 +158,15 @@
             pl.BlockSpec((3, rows, wide), lead),
             pl.BlockSpec((3, edge, wide), lead),
             pl.BlockSpec((3, 3, wide), lead),
-            pl.BlockSpec((modes, groups), lambda n: (0, 0)),
+            pl.BlockSpec((modes, groups), whole),
+            pl.BlockSpec((modes, groups), whole),
         ],
-        out_specs=[
-            pl.BlockSpec((rows, wide), by_block),
-            pl.BlockSpec((modes, wide), by_block),
-            pl.BlockSpec((modes, wide), by_block),
-        ],
-        out_shape=[
-            jax.ShapeDtypeStruct((rows, channels), BF16),
-            jax.ShapeDtypeStruct((modes, channels), F32),
-            jax.ShapeDtypeStruct((modes, channels), F32),
-        ],
+        out_specs=[pl.BlockSpec((rows, wide), lambda n: (0, n))] + [pl.BlockSpec(half, whole)] * 4,
+        out_shape=[jax.ShapeDtypeStruct((rows, channels), BF16)] + [jax.ShapeDtypeStruct(half, F32)] * 4,
         compiler_params=limits(16),
         cost_estimate=cost(4 * rows * terms * channels, 8 * rows * channels),
         name="hyena_ends",
-    )(streams, halo, short_weight, rates)
+    )(streams, halo, short_weight, rates, residues)
 
 
 def hyena_near_body(filters, mixed_ref, rate_ref, res_ref, near_ref, taps_s, u_s):
@@ -218,7 +227,7 @@
     )(mixed, rates, residues)
 
 
-def hyena_out_body(filters, near_ref, x_ref, halo_ref, w_ref, carried_ref, rate_ref, res_ref, out_ref):
+def hyena_out_body(filters, near_ref, x_ref, halo_ref, w_ref, keep_ref, back_ref, rate_ref, out_ref):
     rows = near_ref.shape[0]
     modes, groups = rate_ref.shape
     parts = groups // STEPS // filters
@@ -226,16 +235,16 @@
     lanes = near_ref.shape[1] // parts
     width = lanes // filters
     rates = of_step(rate_ref)
-    coeffs = of_step(res_ref) * jnp.sqrt(2.0 * rates / modes)
     lag = (1 + lax.broadcasted_iota(jnp.int32, (terms, rows), 1)).astype(F32)
     own = same_filter(modes, width, terms, lanes)
+    mine = pl.program_id(0) // (STEPS // 2) == spot()[0]
     for part in range(parts):
         at = slice(part * lanes, (part + 1) * lanes)
-        rate = down(rates, part, filters, rows)
-        powers = (down(coeffs, part, filters, rows) * jnp.exp(-rate * lag)).T
+        powers = jnp.exp(-down(rates, part, filters, rows) * lag).T
         p_high = powers.astype(BF16)
         p_low = (powers - p_high.astype(F32)).astype(BF16)
-        carried = jnp.where(own, jnp.concatenate([carried_ref[:, at]] * filters, axis=0), 0.0)
+        carried = jnp.where(mine, keep_ref[:, at], back_ref[:, at])
+        carried = jnp.where(own, jnp.concatenate([carried] * filters, axis=0), 0.0)
         c_high = carried.astype(BF16)
         c_low = (carried - c_high.astype(F32)).astype(BF16)
         far = (
@@ -247,7 +256,7 @@
         out_ref[:, at] = (query * (near_ref[:, at] + far)).astype(BF16)
 
 
-def hyena_finish(near, streams, halo, short_weight, carried, rates, residues):
+def hyena_finish(near, streams, halo, short_weight, keep, back, rates):
     rows, channels = near.shape
     edge = halo.shape[1]
     modes, groups = rates.shape
@@ -255,8 +264,8 @@
     terms = filters * modes
     wide = channels // STEPS
     by_block = lambda n: (0, n)
+    by_half = lambda n: (0, n % (STEPS // 2))
     lead = lambda n: (0, 0, n)
-    whole = lambda n: (0, 0)
     return pl.pallas_call(
         functools.partial(hyena_out_body, filters),
         grid=(STEPS,),
@@ -265,48 +274,84 @@
             pl.BlockSpec((1, rows, wide), lead),
             pl.BlockSpec((1, edge, wide), lead),
             pl.BlockSpec((3, 3, wide), lead),
-            pl.BlockSpec((modes, wide), by_block),
-            pl.BlockSpec((modes, groups), whole),
-            pl.BlockSpec((modes, groups), whole),
+            pl.BlockSpec((modes, wide), by_half),
+            pl.BlockSpec((modes, wide), by_half),
+            pl.BlockSpec((modes, groups), lambda n: (0, 0)),
         ],
         out_specs=pl.BlockSpec((rows, wide), by_block),
         out_shape=jax.ShapeDtypeStruct((rows, channels), BF16),
         compiler_params=limits(16),
         cost_estimate=cost(6 * rows * terms * channels, 10 * rows * channels),
         name="hyena_finish",
-    )(near, streams, halo, short_weight, carried, rates, residues)
-
-
-def scan_states(ends, rate, rows):
-    half = ends.shape[1] // 2
-    index = lax.axis_index("ctx")
+    )(near, streams, halo, short_weight, keep, back, rates)
+
+
+def small(body, *operands, outs=1):
+    def kernel(*refs):
+        made = body(*(ref[...] for ref in refs[: len(operands)]))
+        for ref, value in zip(refs[len(operands) :], made if outs > 1 else (made,)):
+            ref[...] = value
+
+    shape = pltpu.VMEM(operands[0].shape, operands[0].dtype)
+    made = pl.pallas_call(
+        kernel,
+        in_specs=[VMEM] * len(operands),
+        out_specs=[VMEM] * outs,
+        out_shape=[shape] * outs,
+        compiler_params=limits(4),
+        cost_estimate=cost(operands[0].size, 4 * operands[0].size),
+    )(*operands)
+    return made if outs > 1 else made[0]
+
+
+def scan_states(keep, away, rate, gain, rows):
     count = lax.axis_size("ctx") // ROW
-    core, side = index % 2, index // 2 % 2
-    take = lambda matrix, which: lax.dynamic_slice_in_dim(matrix, which * half, half, 1)
-    rate = take(rate, core)
-    decay = lambda blocks: jnp.exp(-rate * float(rows * blocks))
-    mine = take(ends, core)
-    theirs = flip(take(ends, 1 - core), "ctx", 1)
-    even = jnp.where(core == 0, mine, theirs)
-    odd = jnp.where(core == 0, theirs, mine)
-    chip = decay(1) * even + odd
+    decay = lambda blocks, rate: jnp.exp(-rate * float(rows * blocks))
+
+    def both(mine, theirs, rate):
+        first = spot()[0] == 0
+        even = jnp.where(first, mine, theirs)
+        return decay(1, rate) * even + jnp.where(first, theirs, mine), even
+
+    theirs = flip(away, "ctx", 1)
+    chip, even = small(both, keep, theirs, rate, outs=2)
+
+    def whole(mine, other, rate):
+        first = spot()[1] == 0
+        left = jnp.where(first, mine, other)
+        return decay(2, rate) * left + jnp.where(first, other, mine), left
+
     other = flip(chip, "ctx", 2)
-    left = jnp.where(side == 0, chip, other)
-    total = decay(2) * left + jnp.where(side == 0, other, chip)
+    total, left = small(whole, chip, other, rate, outs=2)
     before = ahead(total, "ctx", ROW)
     reach = 2
     while reach < count:
-        upto = total + decay(ROW) * before
+        upto = small(lambda total, before, rate: total + decay(ROW, rate) * before, total, before, rate)
         earlier = ahead(upto, "ctx", ROW * reach)
-        before = before + decay(ROW * (reach - 1)) * earlier
         reach *= 2
-    before = jnp.where(side == 0, before, decay(2) * before + left)
-    second = decay(1) * before + even
-    keep = jnp.where(core == 0, before, second)
-    back = flip(jnp.where(core == 0, second, before), "ctx", 1)
-    return jnp.concatenate(
-        [jnp.where(core == 0, keep, back), jnp.where(core == 0, back, keep)], axis=1
-    )
+        if reach < count:
+            before = small(
+                lambda before, earlier, rate: before + decay(ROW * (reach // 2 - 1), rate) * earlier,
+                before,
+                earlier,
+                rate,
+            )
+
+    def last(before, earlier, left, even, rate, gain):
+        before = before + decay(ROW * (reach // 2 - 1), rate) * earlier
+        core, side, _, _ = spot()
+        before = jnp.where(side == 0, before, decay(2, rate) * before + left)
+        second = decay(1, rate) * before + even
+        return (
+            gain * jnp.where(core == 0, before, second),
+            gain * jnp.where(core == 0, second, before),
+        )
+
+    if count == 2:
+        earlier = jnp.zeros_like(before)
+    if count > 1:
+        mine, away = small(last, before, earlier, left, even, rate, gain, outs=2)
+    return mine, flip(away, "ctx", 1)
 
 
 def lanes_from(start, size):
@@ -334,11 +379,11 @@
         in_specs=[HBM, HBM],
         out_specs=[VMEM, VMEM],
         out_shape=[
-            jax.ShapeDtypeStruct((count, rows, channels // 2), attn.dtype),
-            jax.ShapeDtypeStruct((count, EDGE, channels), hyena.dtype),
+            pltpu.VMEM((count, rows, channels // 2), attn.dtype),
+            pltpu.VMEM((count, EDGE, channels), hyena.dtype),
         ],
         scratch_shapes=[pltpu.SemaphoreType.DMA((2,))],
-        compiler_params=pltpu.CompilerParams(vmem_limit_bytes=ALL_VMEM - (18 << 17)),
+        compiler_params=pltpu.CompilerParams(vmem_limit_bytes=ALL_VMEM - (26 << 17)),
         cost_estimate=cost(0, 4 * count * rows * channels // 2),
         name="front",
     )(attn, hyena)
@@ -357,7 +402,7 @@
 
 def pack(streams, theirs, first, amount):
     _, rows, half = theirs.shape
-    shape = jax.ShapeDtypeStruct((2, 3 - first, rows, half // 2), BF16)
+    shape = pltpu.VMEM((2, 3 - first, rows, half // 2), BF16)
     return pl.pallas_call(
         functools.partial(pack_body, first),
         in_specs=[VMEM, VMEM],
@@ -367,6 +412,27 @@
         cost_estimate=cost(0, 8 * amount * rows * half),
         name="pack",
     )(streams, theirs)
+
+
+def odd_body(wanted, pairs, out_ref, sem):
+    @pl.when(spot()[1] == wanted)
+    def _():
+        copy = pltpu.make_async_copy(pairs.at[0:1], out_ref, sem)
+        copy.start()
+        copy.wait()
+
+
+def odd(pairs, wanted):
+    return pl.pallas_call(
+        functools.partial(odd_body, wanted),
+        in_specs=[ANY],
+        out_specs=VMEM,
+        out_shape=pltpu.VMEM((1,) + pairs.shape[1:], pairs.dtype),
+        scratch_shapes=[pltpu.SemaphoreType.DMA],
+        compiler_params=limits(4),
+        cost_estimate=cost(0, pairs.size * 2),
+        name="odd",
+    )(pairs)
 
 
 def contig_start(docs_ref, position):
@@ -622,15 +688,15 @@
     swap = flip(swap, "ctx", 2)
     olds = (
         ahead(cross, "ctx", ROW, 0, ROW, 0),
-        ahead(own[:1], "ctx", ROW, 0, ROW, 0),
+        ahead(odd(own, 0), "ctx", ROW, 0, ROW, 0),
         ahead(own, "ctx", ROW, 0, ROW, 1),
-        ahead(cross[:1], "ctx", ROW, 0, ROW, 1),
+        ahead(odd(cross, 1), "ctx", ROW, 0, ROW, 1),
     )
 
-    mixed, ends, wide = hyena_ends(inner, edge, short_weight, rates)
+    mixed, keep, away, wide, gain = hyena_ends(inner, edge, short_weight, rates, residues)
     near = hyena_near(mixed, rates, residues)
-    carried = scan_states(ends, wide, rows)
-    hyena_out = hyena_finish(near, inner, edge, short_weight, carried, rates, residues)
+    keep, back = scan_states(keep, away, wide, gain, rows)
+    hyena_out = hyena_finish(near, inner, edge, short_weight, keep, back, rates)
 
     acc, top, below = attend(doc_lengths, streams, theirs, swap, own, cross)
     made = attend_last(doc_lengths, streams, theirs, swap, olds, acc, top, below)

time: 85.7 us -> 87 us (1.015)
  the two profiles are of different devices: /device:TPU:21 before, /device:TPU:0 now
where the time goes in v1:
time: 87 us; the launch traced here: 86.7 us
  starting transfers between devices  38.8 us (45%)
  Pallas kernels  24.7 us (28%)
  waiting for transfers between devices  22.2 us (26%)
  between operations  0.96 us (1%)
    ppermute x9, starting transfers between devices, ahead(): return lax.ppermute(value, axis, pairs)  31.8 us
    ppermute x9, waiting for transfers between devices, ahead(): return lax.ppermute(value, axis, pairs)  16.6 us
    pallas_call x1, Pallas kernels, attend(): pl.pallas_call(attend_body, in_specs=[SMEM] + [ANY] * 5, out_specs=[VMEM]...  7.39 us
    ppermute x8, starting transfers between devices, flip(): return lax.ppermute(value, axis, [(at, at ^ bit) for at in range(count)])  6.99 us
    ppermute x8, waiting for transfers between devices, flip(): return lax.ppermute(value, axis, [(at, at ^ bit) for at in range(count)])  5.58 us
    pallas_call x1, Pallas kernels, hyena_ends(): pl.pallas_call(functools.partial(hyena_ends_body, filters), grid=(STEPS,)...  4.99 us
    pallas_call x1, Pallas kernels, hyena_near(): pl.pallas_call(functools.partial(hyena_near_body, filters), grid=(STEPS,)...  4.34 us
    pallas_call x1, Pallas kernels, hyena_finish(): pl.pallas_call(functools.partial(hyena_out_body, filters), grid=(STEPS,),...  3.17 us
  transfers between devices with their start and end apart: 17, of which 6 were waited for; matrix products, arithmetic and copies ran while one was open for 0% of the time, Pallas kernels for 26%

profile of v1, /device:TPU:0, one launch (start us, length us, event | category | flops | bytes accessed | tf_op | source)
XLA Modules:
  0.0 86.7 jit_solution(3159734547498869904)
XLA Ops:
  0.6 1.3 %front.1 = (bf16[3,128,1024]{2,1,0:T(8,128)(2,1)S(1)}, bf16[3,8,2048]{2,1,0:T(8,128)(2,1)S(1)}) custom-call(bf16[3,128,2048]{2,1,0:T(8,128)(2,1)} %bitcast.4, bf16[3,128,2048]{2,1,0:T(8,128)(2,1)} %bitcast.9), custom_call_target="tpu_custom_call" | custom-call | bytes 1572864 | tf_op jit(solution)/shard_map/front/pallas_call | solution.py:377
  1.9 0.6 collective-permute-start.6
  2.5 1.9 %collective-permute-done.6.theirs_ref.theirs = bf16[3,128,1024]{2,1,0:T(8,128)(2,1)S(1)} collective-permute-done((bf16[3,128,1024]{2,1,0:T(8,128)(2,1)S(1)}, bf16[3,128,1024]{2,1,0:T(8,128)(2,1)S(1)}, u32[]{:S(2)}, u32[]{:S(2)}) %collective-permute-start.6) | collective-permute-done | bytes 786464 | tf_op jit(solution)/shard_map/ppermute | solution.py:23
  4.4 0.1 pack.3
  4.5 4.9 %collective-permute-start.10 = (bf16[2,2,128,512]{3,2,1,0:T(8,128)(2,1)S(1)}, bf16[2,2,128,512]{3,2,1,0:T(8,128)(2,1)S(1)}, u32[]{:S(2)}, u32[]{:S(2)}) collective-permute-start(bf16[2,2,128,512]{3,2,1,0:T(8,128)(2,1)S(1)} %get-tuple-element.38), channel_id=1, source_target_pairs={{0,4},{1,5},{2,6},{3,7},{4,8},{5,9},{6,10},{7,11},{8,12},{9,13},{1... | collective-permute-start | bytes 1572872 | tf_op jit(solution)/shard_map/ppermute | solution.py:37
  9.4 4.6 %collective-permute-start.8 = (bf16[2,2,128,512]{3,2,1,0:T(8,128)(2,1)S(1)}, bf16[2,2,128,512]{3,2,1,0:T(8,128)(2,1)S(1)}, u32[]{:S(2)}, u32[]{:S(2)}) collective-permute-start(bf16[2,2,128,512]{3,2,1,0:T(8,128)(2,1)S(1)} %get-tuple-element.37), channel_id=1, source_target_pairs={{0,6},{1,7},{2,4},{3,5},{4,10},{5,11},{6,8},{7,9},{8,14},{9,15},{1... | collective-permute-start | bytes 1572872 | tf_op jit(solution)/shard_map/ppermute | solution.py:37
  14.0 0.1 pack.2
  14.1 0.6 collective-permute-start.7
  14.6 1.3 %collective-permute-start = (bf16[3,8,2048]{2,1,0:T(8,128)(2,1)S(1)}, bf16[3,8,2048]{2,1,0:T(8,128)(2,1)S(1)}, u32[]{:S(2)}, u32[]{:S(2)}) collective-permute-start(bf16[3,8,2048]{2,1,0:T(8,128)(2,1)S(1)} %get-tuple-element.24), channel_id=1, source_target_pairs={{0,1},{1,2},{2,3},{3,4},{4,5},{5,6},{6,7},{7,8},{8,9},{9,10},{10,1... | collective-permute-start | bytes 294920 | tf_op jit(solution)/shard_map/ppermute | solution.py:37
  15.9 5.7 %collective-permute-done.10.pairs.own = bf16[2,2,128,512]{3,2,1,0:T(8,128)(2,1)S(1)} collective-permute-done((bf16[2,2,128,512]{3,2,1,0:T(8,128)(2,1)S(1)}, bf16[2,2,128,512]{3,2,1,0:T(8,128)(2,1)S(1)}, u32[]{:S(2)}, u32[]{:S(2)}) %collective-permute-start.10) | collective-permute-done | bytes 524320 | tf_op jit(solution)/shard_map/ppermute | solution.py:37
  21.6 0.7 collective-permute-start.12
  22.3 9.8 %collective-permute-done.8.pairs.cross = bf16[2,2,128,512]{3,2,1,0:T(8,128)(2,1)S(1)} collective-permute-done((bf16[2,2,128,512]{3,2,1,0:T(8,128)(2,1)S(1)}, bf16[2,2,128,512]{3,2,1,0:T(8,128)(2,1)S(1)}, u32[]{:S(2)}, u32[]{:S(2)}) %collective-permute-start.8) | collective-permute-done | bytes 524320 | tf_op jit(solution)/shard_map/ppermute | solution.py:37
  32.1 0.7 collective-permute-start.9
  32.8 5.0 %hyena_ends.1 = (bf16[128,2048]{1,0:T(8,128)(2,1)S(1)}, f32[16,1024]{1,0:T(8,128)S(1)}, f32[16,1024]{1,0:T(8,128)S(1)}, f32[16,1024]{1,0:T(8,128)S(1)}, f32[16,1024]{1,0:T(8,128)S(1)}) custom-call(bf16[3,128,2048]{2,1,0:T(8,128)(2,1)S(1)} %bitcast.10, bf16[3,8,2048]{2,1,0:T(8,128)(2,1)S(1)} %collective-permute-done.halo_ref, f32[3,3,2048]{2,1,0:T(4,128)S(1)} %copy-done.2, ...), custom_call_target="tpu_custom_call" | custom-call | flops 134217728 | bytes 2097152 | tf_op jit(solution)/shard_map/hyena_ends/pallas_call | solution.py:154
  37.8 0.1 collective-permute-start.1
  37.9 1.2 %collective-permute-done.1.refs_1_ = f32[16,1024]{1,0:T(8,128)S(1)} collective-permute-done((f32[16,1024]{1,0:T(8,128)S(1)}, f32[16,1024]{1,0:T(8,128)S(1)}, u32[]{:S(2)}, u32[]{:S(2)}) %collective-permute-start.1) | collective-permute-done | bytes 65568 | tf_op jit(solution)/shard_map/ppermute | solution.py:23
  39.2 2.4 %collective-permute-start.2 = (f32[16,1024]{1,0:T(8,128)S(1)}, f32[16,1024]{1,0:T(8,128)S(1)}, u32[]{:S(2)}, u32[]{:S(2)}) collective-permute-start(f32[16,1024]{1,0:T(8,128)S(1)} %get-tuple-element.29.refs_0_), channel_id=1, source_target_pairs={{0,2},{1,3},{2,0},{3,1},{4,6},{5,7},{6,4},{7,5},{8,10},{9,11},{10,... | collective-permute-start | bytes 196616 | tf_op jit(solution)/shard_map/ppermute | solution.py:23
  41.6 2.4 %collective-permute-done.2.refs_1_ = f32[16,1024]{1,0:T(8,128)S(1)} collective-permute-done((f32[16,1024]{1,0:T(8,128)S(1)}, f32[16,1024]{1,0:T(8,128)S(1)}, u32[]{:S(2)}, u32[]{:S(2)}) %collective-permute-start.2) | collective-permute-done | bytes 65568 | tf_op jit(solution)/shard_map/ppermute | solution.py:23
  44.0 13.9 %collective-permute-start.3 = (f32[16,1024]{1,0:T(8,128)S(1)}, f32[16,1024]{1,0:T(8,128)S(1)}, u32[]{:S(2)}, u32[]{:S(2)}) collective-permute-start(f32[16,1024]{1,0:T(8,128)S(1)} %get-tuple-element.30.refs_0_), channel_id=1, source_target_pairs={{0,4},{1,5},{2,6},{3,7},{4,8},{5,9},{6,10},{7,11},{8,12},{9,13},{1... | collective-permute-start | bytes 196616 | tf_op jit(solution)/shard_map/ppermute | solution.py:37
  58.0 0.7 collective-permute-start.11
  58.7 1.1 %collective-permute-done.3.refs_1_.refs_0_ = f32[16,1024]{1,0:T(8,128)S(1)} collective-permute-done((f32[16,1024]{1,0:T(8,128)S(1)}, f32[16,1024]{1,0:T(8,128)S(1)}, u32[]{:S(2)}, u32[]{:S(2)}) %collective-permute-start.3) | collective-permute-done | bytes 65568 | tf_op jit(solution)/shard_map/ppermute | solution.py:37
  59.8 0.7 collective-permute-start.13
  60.5 4.5 %collective-permute-start.4 = (f32[16,1024]{1,0:T(8,128)S(1)}, f32[16,1024]{1,0:T(8,128)S(1)}, u32[]{:S(2)}, u32[]{:S(2)}) collective-permute-start(f32[16,1024]{1,0:T(8,128)S(1)} %shard_map.79), channel_id=1, source_target_pairs={{0,8},{1,9},{2,10},{3,11},{4,12},{5,13},{6,14},{7,15},{16,24},{17,... | collective-permute-start | bytes 196616 | tf_op jit(solution)/shard_map/ppermute | solution.py:37
  65.0 7.4 %attend.1 = (f32[512,512]{1,0:T(8,128)S(1)}, f32[512,512]{1,0:T(8,128)S(1)}, f32[512,512]{1,0:T(8,128)S(1)}) custom-call(s32[4]{0:T(128)S(1)} %copy-done.5, bf16[3,128,2048]{2,1,0:T(8,128)(2,1)S(1)} %bitcast.7, bf16[3,128,1024]{2,1,0:T(8,128)(2,1)S(1)} %collective-permute-done.6.theirs_ref.theirs, bf16[2,3,128,512]{3,2,1,0:T(8,128)(2,1)S(1)} %collective-permute-done.7.swap, ...), custom_call_target="tpu_custom_call" | custom-call | flops 872415232 | bytes 3670016 | tf_op jit(solution)/shard_map/attend/pallas_call | solution.py:536
  72.5 2.4 %attend_last.1 = (bf16[128,512]{1,0:T(8,128)(2,1)S(1)}, bf16[128,512]{1,0:T(8,128)(2,1)S(1)}, bf16[128,512]{1,0:T(8,128)(2,1)S(1)}, bf16[128,512]{1,0:T(8,128)(2,1)S(1)}) custom-call(s32[4]{0:T(128)S(1)} %copy-done.5, bf16[3,128,2048]{2,1,0:T(8,128)(2,1)S(1)} %bitcast.8, bf16[3,128,1024]{2,1,0:T(8,128)(2,1)S(1)} %collective-permute-done.6.theirs_ref.theirs, ...), custom_call_target="tpu_custom_call" | custom-call | flops 201326592 | bytes 3145728 | tf_op jit(solution)/shard_map/attend_last/pallas_call | solution.py:635
  74.9 0.1 collective-permute-start.14
  75.0 3.0 %collective-permute-start.15 = (bf16[128,512]{1,0:T(8,128)(2,1)S(1)}, bf16[128,512]{1,0:T(8,128)(2,1)S(1)}, u32[]{:S(2)}, u32[]{:S(2)}) collective-permute-start(bf16[128,512]{1,0:T(8,128)(2,1)S(1)} %get-tuple-element.44), channel_id=1, source_target_pairs={{0,2},{1,3},{2,0},{3,1},{4,6},{5,7},{6,4},{7,5},{8,10},{9,11},{10,... | collective-permute-start | bytes 393224 | tf_op jit(solution)/shard_map/ppermute | solution.py:23
  78.0 0.1 shard_map.80
  78.1 0.2 collective-permute-start.5
  78.3 4.3 %hyena_near.1.near_ref = f32[128,2048]{1,0:T(8,128)S(1)} custom-call(bf16[128,2048]{1,0:T(8,128)(2,1)S(1)} %get-tuple-element.25.mixed_ref, f32[16,128]{1,0:T(8,128)S(1)} %bitcast.13, f32[16,128]{1,0:T(8,128)S(1)} %bitcast.16), custom_call_target="tpu_custom_call" | custom-call | flops 536870912 | bytes 3145728 | tf_op jit(solution)/shard_map/hyena_near/pallas_call | solution.py:210
  82.7 3.2 %hyena_finish.1 = bf16[128,2048]{1,0:T(8,128)(2,1)} custom-call(f32[128,2048]{1,0:T(8,128)S(1)} %hyena_near.1.near_ref, bf16[3,128,2048]{2,1,0:T(8,128)(2,1)S(1)} %bitcast.11, bf16[3,8,2048]{2,1,0:T(8,128)(2,1)S(1)} %collective-permute-done.halo_ref, f32[3,3,2048]{2,1,0:T(4,128)S(1)} %copy-done.2, f32[16,1024]{1,0:T(8,128)S(1)} %get-tuple-element.34.keep_ref, ...), custom_call_target="tpu_custom_call" | custom-call | flops 201326592 | bytes 2621440 | tf_op jit(solution)/shard_map/hyena_finish/pallas_call | solution.py:269
  85.9 0.8 assemble.1
  (29 shorter events, 0.2 us)
Async XLA Ops:
  0.6 3.8 %copy-start = (bf16[128,3,2048]{2,0,1:T(8,128)(2,1)S(1)}, bf16[128,3,2048]{2,0,1:T(8,128)(2,1)}, u32[]{:S(2)}) copy-start(bf16[128,3,2048]{2,0,1:T(8,128)(2,1)} %param.10) | copy-start | bytes 4718596
  1.9 2.5 %collective-permute-start.6 = (bf16[3,128,1024]{2,1,0:T(8,128)(2,1)S(1)}, bf16[3,128,1024]{2,1,0:T(8,128)(2,1)S(1)}, u32[]{:S(2)}, u32[]{:S(2)}) collective-permute-start(bf16[3,128,1024]{2,1,0:T(8,128)(2,1)S(1)} %get-tuple-element.36), channel_id=1, source_target_pairs={{0,1},{1,0},{2,3},{3,2},{4,5},{5,4},{6,7},{7,6},{8,9},{9,8},{10,11... | collective-permute-start | bytes 2359304 | tf_op jit(solution)/shard_map/ppermute | solution.py:23
  4.5 17.1 %collective-permute-start.10 = (bf16[2,2,128,512]{3,2,1,0:T(8,128)(2,1)S(1)}, bf16[2,2,128,512]{3,2,1,0:T(8,128)(2,1)S(1)}, u32[]{:S(2)}, u32[]{:S(2)}) collective-permute-start(bf16[2,2,128,512]{3,2,1,0:T(8,128)(2,1)S(1)} %get-tuple-element.38), channel_id=1, source_target_pairs={{0,4},{1,5},{2,6},{3,7},{4,8},{5,9},{6,10},{7,11},{8,12},{9,13},{1... | collective-permute-start | bytes 1572872 | tf_op jit(solution)/shard_map/ppermute | solution.py:37
  9.4 23.4 %copy-start.1 = (bf16[128,3,2048]{2,0,1:T(8,128)(2,1)S(1)}, bf16[128,3,2048]{2,0,1:T(8,128)(2,1)}, u32[]{:S(2)}) copy-start(bf16[128,3,2048]{2,0,1:T(8,128)(2,1)} %param.6) | copy-start | bytes 4718596
  9.4 23.4 %copy-start.2 = (f32[3,3,2048]{2,1,0:T(4,128)S(1)}, f32[3,3,2048]{2,1,0:T(4,128)}, u32[]{:S(2)}) copy-start(f32[3,3,2048]{2,1,0:T(4,128)} %w_ref.3) | copy-start | bytes 221188
  9.4 23.4 %copy-start.3 = (f32[128,16]{0,1:T(8,128)S(1)}, f32[128,16]{0,1:T(8,128)}, u32[]{:S(2)}) copy-start(f32[128,16]{0,1:T(8,128)} %param.8) | copy-start | bytes 24580
  9.4 23.4 %copy-start.4 = (f32[128,16]{0,1:T(8,128)S(1)}, f32[128,16]{0,1:T(8,128)}, u32[]{:S(2)}) copy-start(f32[128,16]{0,1:T(8,128)} %param.9) | copy-start | bytes 24580
  9.4 22.7 %collective-permute-start.8 = (bf16[2,2,128,512]{3,2,1,0:T(8,128)(2,1)S(1)}, bf16[2,2,128,512]{3,2,1,0:T(8,128)(2,1)S(1)}, u32[]{:S(2)}, u32[]{:S(2)}) collective-permute-start(bf16[2,2,128,512]{3,2,1,0:T(8,128)(2,1)S(1)} %get-tuple-element.37), channel_id=1, source_target_pairs={{0,6},{1,7},{2,4},{3,5},{4,10},{5,11},{6,8},{7,9},{8,14},{9,15},{1... | collective-permute-start | bytes 1572872 | tf_op jit(solution)/shard_map/ppermute | solution.py:37
  14.1 46.5 %collective-permute-start.7 = (bf16[2,3,128,512]{3,2,1,0:T(8,128)(2,1)S(1)}, bf16[2,3,128,512]{3,2,1,0:T(8,128)(2,1)S(1)}, u32[]{:S(2)}, u32[]{:S(2)}) collective-permute-start(bf16[2,3,128,512]{3,2,1,0:T(8,128)(2,1)S(1)} %pack.2), channel_id=1, source_target_pairs={{0,2},{1,3},{2,0},{3,1},{4,6},{5,7},{6,4},{7,5},{8,10},{9,11},{10,... | collective-permute-start | bytes 2359304 | tf_op jit(solution)/shard_map/ppermute | solution.py:23
  14.6 18.1 %collective-permute-start = (bf16[3,8,2048]{2,1,0:T(8,128)(2,1)S(1)}, bf16[3,8,2048]{2,1,0:T(8,128)(2,1)S(1)}, u32[]{:S(2)}, u32[]{:S(2)}) collective-permute-start(bf16[3,8,2048]{2,1,0:T(8,128)(2,1)S(1)} %get-tuple-element.24), channel_id=1, source_target_pairs={{0,1},{1,2},{2,3},{3,4},{4,5},{5,6},{6,7},{7,8},{8,9},{9,10},{10,1... | collective-permute-start | bytes 294920 | tf_op jit(solution)/shard_map/ppermute | solution.py:37
  21.6 50.8 %collective-permute-start.12 = (bf16[2,2,128,512]{3,2,1,0:T(8,128)(2,1)S(1)}, bf16[2,2,128,512]{3,2,1,0:T(8,128)(2,1)S(1)}, u32[]{:S(2)}, u32[]{:S(2)}) collective-permute-start(bf16[2,2,128,512]{3,2,1,0:T(8,128)(2,1)S(1)} %collective-permute-done.10.pairs.own), channel_id=1, source_target_pairs={{6,10},{7,11},{10,14},{11,15},{22,26},{23,27},{26,30},{27,31}} | collective-permute-start | bytes 1572872 | tf_op jit(solution)/shard_map/ppermute | solution.py:37
  32.1 40.4 %collective-permute-start.9 = (bf16[2,2,128,512]{3,2,1,0:T(8,128)(2,1)S(1)}, bf16[2,2,128,512]{3,2,1,0:T(8,128)(2,1)S(1)}, u32[]{:S(2)}, u32[]{:S(2)}) collective-permute-start(bf16[2,2,128,512]{3,2,1,0:T(8,128)(2,1)S(1)} %collective-permute-done.8.pairs.cross), channel_id=1, source_target_pairs={{4,8},{5,9},{8,12},{9,13},{20,24},{21,25},{24,28},{25,29}} | collective-permute-start | bytes 1572872 | tf_op jit(solution)/shard_map/ppermute | solution.py:37
  32.8 32.2 %copy-start.5 = (s32[4]{0:T(128)S(1)}, s32[4]{0:T(128)}, u32[]{:S(2)}) copy-start(s32[4]{0:T(128)} %docs_ref.3) | copy-start | bytes 52
  37.8 1.3 %collective-permute-start.1 = (f32[16,1024]{1,0:T(8,128)S(1)}, f32[16,1024]{1,0:T(8,128)S(1)}, u32[]{:S(2)}, u32[]{:S(2)}) collective-permute-start(f32[16,1024]{1,0:T(8,128)S(1)} %get-tuple-element.27), channel_id=1, source_target_pairs={{0,1},{1,0},{2,3},{3,2},{4,5},{5,4},{6,7},{7,6},{8,9},{9,8},{10,11... | collective-permute-start | bytes 196616 | tf_op jit(solution)/shard_map/ppermute | solution.py:23
  39.2 4.8 %collective-permute-start.2 = (f32[16,1024]{1,0:T(8,128)S(1)}, f32[16,1024]{1,0:T(8,128)S(1)}, u32[]{:S(2)}, u32[]{:S(2)}) collective-permute-start(f32[16,1024]{1,0:T(8,128)S(1)} %get-tuple-element.29.refs_0_), channel_id=1, source_target_pairs={{0,2},{1,3},{2,0},{3,1},{4,6},{5,7},{6,4},{7,5},{8,10},{9,11},{10,... | collective-permute-start | bytes 196616 | tf_op jit(solution)/shard_map/ppermute | solution.py:23
  44.0 15.8 %collective-permute-start.3 = (f32[16,1024]{1,0:T(8,128)S(1)}, f32[16,1024]{1,0:T(8,128)S(1)}, u32[]{:S(2)}, u32[]{:S(2)}) collective-permute-start(f32[16,1024]{1,0:T(8,128)S(1)} %get-tuple-element.30.refs_0_), channel_id=1, source_target_pairs={{0,4},{1,5},{2,6},{3,7},{4,8},{5,9},{6,10},{7,11},{8,12},{9,13},{1... | collective-permute-start | bytes 196616 | tf_op jit(solution)/shard_map/ppermute | solution.py:37
  58.0 14.4 %collective-permute-start.11 = (bf16[1,2,128,512]{3,2,1,0:T(8,128)(2,1)S(1)}, bf16[1,2,128,512]{3,2,1,0:T(8,128)(2,1)S(1)}, u32[]{:S(2)}, u32[]{:S(2)}) collective-permute-start(bf16[1,2,128,512]{3,2,1,0:T(8,128)(2,1)S(1)} %odd.2), channel_id=1, source_target_pairs={{4,8},{5,9},{8,12},{9,13},{20,24},{21,25},{24,28},{25,29}} | collective-permute-start | bytes 786440 | tf_op jit(solution)/shard_map/ppermute | solution.py:37
  59.8 12.6 %collective-permute-start.13 = (bf16[1,2,128,512]{3,2,1,0:T(8,128)(2,1)S(1)}, bf16[1,2,128,512]{3,2,1,0:T(8,128)(2,1)S(1)}, u32[]{:S(2)}, u32[]{:S(2)}) collective-permute-start(bf16[1,2,128,512]{3,2,1,0:T(8,128)(2,1)S(1)} %odd.3), channel_id=1, source_target_pairs={{6,10},{7,11},{10,14},{11,15},{22,26},{23,27},{26,30},{27,31}} | collective-permute-start | bytes 786440 | tf_op jit(solution)/shard_map/ppermute | solution.py:37
  60.5 17.5 %collective-permute-start.4 = (f32[16,1024]{1,0:T(8,128)S(1)}, f32[16,1024]{1,0:T(8,128)S(1)}, u32[]{:S(2)}, u32[]{:S(2)}) collective-permute-start(f32[16,1024]{1,0:T(8,128)S(1)} %shard_map.79), channel_id=1, source_target_pairs={{0,8},{1,9},{2,10},{3,11},{4,12},{5,13},{6,14},{7,15},{16,24},{17,... | collective-permute-start | bytes 196616 | tf_op jit(solution)/shard_map/ppermute | solution.py:37
  74.9 11.0 %collective-permute-start.14 = (bf16[128,512]{1,0:T(8,128)(2,1)S(1)}, bf16[128,512]{1,0:T(8,128)(2,1)S(1)}, u32[]{:S(2)}, u32[]{:S(2)}) collective-permute-start(bf16[128,512]{1,0:T(8,128)(2,1)S(1)} %get-tuple-element.43), channel_id=1, source_target_pairs={{0,1},{1,0},{2,3},{3,2},{4,5},{5,4},{6,7},{7,6},{8,9},{9,8},{10,11... | collective-permute-start | bytes 393224 | tf_op jit(solution)/shard_map/ppermute | solution.py:23
  75.0 10.9 %collective-permute-start.15 = (bf16[128,512]{1,0:T(8,128)(2,1)S(1)}, bf16[128,512]{1,0:T(8,128)(2,1)S(1)}, u32[]{:S(2)}, u32[]{:S(2)}) collective-permute-start(bf16[128,512]{1,0:T(8,128)(2,1)S(1)} %get-tuple-element.44), channel_id=1, source_target_pairs={{0,2},{1,3},{2,0},{3,1},{4,6},{5,7},{6,4},{7,5},{8,10},{9,11},{10,... | collective-permute-start | bytes 393224 | tf_op jit(solution)/shard_map/ppermute | solution.py:23
  78.0 7.9 %collective-permute-start.16 = (bf16[128,512]{1,0:T(8,128)(2,1)S(1)}, bf16[128,512]{1,0:T(8,128)(2,1)S(1)}, u32[]{:S(2)}, u32[]{:S(2)}) collective-permute-start(bf16[128,512]{1,0:T(8,128)(2,1)S(1)} %get-tuple-element.45), channel_id=1, source_target_pairs={{0,3},{1,2},{2,1},{3,0},{4,7},{5,6},{6,5},{7,4},{8,11},{9,10},{10,... | collective-permute-start | bytes 393224 | tf_op jit(solution)/shard_map/ppermute | solution.py:23
  78.1 4.6 %collective-permute-start.5 = (f32[16,1024]{1,0:T(8,128)S(1)}, f32[16,1024]{1,0:T(8,128)S(1)}, u32[]{:S(2)}, u32[]{:S(2)}) collective-permute-start(f32[16,1024]{1,0:T(8,128)S(1)} %get-tuple-element.35), channel_id=1, source_target_pairs={{0,1},{1,0},{2,3},{3,2},{4,5},{5,4},{6,7},{7,6},{8,9},{9,8},{10,11... | collective-permute-start | bytes 196616 | tf_op jit(solution)/shard_map/ppermute | solution.py:23

commit v2 on v1

--- a/solution.py
+++ b/solution.py
@@ -97,7 +97,7 @@
 
 
 def hyena_ends_body(
-    filters, x_ref, halo_ref, w_ref, rate_ref, res_ref, mixed_ref, keep_ref, away_ref, wide_ref, gain_ref
+    filters, x_ref, halo_ref, w_ref, rate_ref, res_ref, mixed_ref, keep_ref, away_ref, wide_ref, gain_ref, all_s
 ):
     rows = x_ref.shape[1]
     modes, groups = rate_ref.shape
@@ -111,10 +111,8 @@
     own = same_filter(modes, width, terms, lanes)
     pick = lambda matrix: jnp.sum(jnp.where(own, matrix, 0.0).reshape(filters, modes, lanes), axis=0)
     step = pl.program_id(0)
-    mine = step // (STEPS // 2) == spot()[0]
     for part in range(parts):
         at = slice(part * lanes, (part + 1) * lanes)
-        there = pl.ds(pl.multiple_of((step % (STEPS // 2)) * (parts * lanes) + part * lanes, lanes), lanes)
         key, value = (feature(x_ref[n, :, at], halo_ref[n, :, at], w_ref, n, at) for n in (1, 2))
         mixed = (key * value).astype(BF16)
         mixed_ref[:, at] = mixed
@@ -122,20 +120,22 @@
         powers = jnp.exp(-rate * lag)
         high = powers.astype(BF16)
         low = (powers - high.astype(F32)).astype(BF16)
-        ends = pick(
-            jnp.dot(high, mixed, preferred_element_type=F32)
-            + jnp.dot(low, mixed, preferred_element_type=F32)
+        ends = jnp.dot(high, mixed, preferred_element_type=F32) + jnp.dot(
+            low, mixed, preferred_element_type=F32
         )
-
-        @pl.when(mine)
-        def _():
-            keep_ref[:, there] = ends
-            wide_ref[:, there] = pick(rate)
-            gain_ref[:, there] = pick(down(coeffs, part, filters, rows))
-
-        @pl.when(jnp.logical_not(mine))
-        def _():
-            away_ref[:, there] = ends
+        all_s[0, step, :, at] = pick(ends)
+        all_s[1, step, :, at] = pick(rate)
+        all_s[2, step, :, at] = pick(down(coeffs, part, filters, rows))
+
+    @pl.when(step == STEPS - 1)
+    def _():
+        core = spot()[0]
+        half = STEPS // 2
+        for n in range(half):
+            at = slice(n * parts * lanes, (n + 1) * parts * lanes)
+            away_ref[:, at] = all_s[0, (1 - core) * half + n]
+            for table, out in enumerate((keep_ref, wide_ref, gain_ref)):
+                out[:, at] = all_s[table, core * half + n]
 
 
 STEPS = 4
@@ -163,6 +163,7 @@
         ],
         out_specs=[pl.BlockSpec((rows, wide), lambda n: (0, n))] + [pl.BlockSpec(half, whole)] * 4,
         out_shape=[jax.ShapeDtypeStruct((rows, channels), BF16)] + [jax.ShapeDtypeStruct(half, F32)] * 4,
+        scratch_shapes=[pltpu.VMEM((3, STEPS, modes, wide), F32)],
         compiler_params=limits(16),
         cost_estimate=cost(4 * rows * terms * channels, 8 * rows * channels),
         name="hyena_ends",
@@ -444,90 +445,96 @@
     return first
 
 
-def row_part(streams, theirs, swap, slot, stream, quarter):
+def row_part(streams, theirs, swap, slot, stream, head, quarter):
     core, side, _, _ = spot()
-    if slot == 0:
-        return streams.at[stream, :, lanes_from(2 * core + side, quarter)]
-    if slot == 1:
-        return theirs.at[stream, :, lanes_from(side, quarter)]
-    return swap.at[slot - 2, stream]
+    if slot < 2:
+        start = (side if slot else 2 * core + side) * quarter + head * HEAD
+        lanes = pl.ds(pl.multiple_of(start, HEAD), HEAD)
+        return theirs[stream, :, lanes] if slot else streams[stream, :, lanes]
+    return swap[slot - 2, stream, :, head * HEAD : (head + 1) * HEAD]
 
 
 SCALE = math.log2(math.e) / math.sqrt(HEAD)
 
 
-KEYS = 256
-GROUP = 2
 CHUNK = 32
 
 
-def attend_body(docs_ref, streams, theirs, swap, own, cross, acc_ref, m_ref, l_ref, q_s, k_s, v_s, bias_s, s_s, p_s, sems):
+def softmax_group(queries, keys, values, bias, turn, s_s, p_s, keep):
+    tall, rows = queries.shape[0], keys[0].shape[0]
+    width = len(keys) * rows
+    for n in range(0, len(keys), 2):
+        s_s[turn, 0:tall, n * rows : (n + 2) * rows] = lax.dot_general(
+            queries,
+            jnp.concatenate(keys[n : n + 2], axis=0),
+            (((1,), (1,)), ((), ())),
+            preferred_element_type=F32,
+        )
+    for m in range(0, tall, CHUNK):
+        some = slice(m, m + CHUNK)
+        top = None
+        parts = []
+        for n in range(0, width, LANES):
+            part = s_s[turn, some, n : n + LANES] + bias[some, n : n + LANES]
+            parts.append(part)
+            top = part if top is None else jnp.maximum(top, part)
+        top = jnp.broadcast_to(jnp.max(top, axis=1, keepdims=True), (CHUNK, LANES))
+        below = jnp.zeros((CHUNK, LANES), F32)
+        for n, part in enumerate(parts):
+            weight = jnp.exp2((part - top) * SCALE)
+            below = below + weight
+            p_s[turn, some, n * LANES : (n + 1) * LANES] = weight.astype(BF16)
+        keep(m, top, jnp.broadcast_to(jnp.sum(below, axis=1, keepdims=True), (CHUNK, LANES)))
+    return jnp.dot(
+        p_s[turn, 0:tall, 0:width], jnp.concatenate(values, axis=0), preferred_element_type=F32
+    )
+
+
+def attend_body(docs_ref, streams, theirs, swap, own, cross, acc_ref, m_ref, l_ref, bias_s, s_s, p_s):
     _, side, place, row = spot()
-    rows, quarter = q_s.shape[0] // ROW, q_s.shape[1]
+    rows, quarter = own.shape[2:]
     base = row * (ROW * rows)
-    copies = []
-
-    def bring(source, target):
-        copies.append(pltpu.make_async_copy(source, target, sems.at[len(copies)]))
-        copies[-1].start()
-
-    for n in range(2):
-        for old, which in ((own, side), (cross, 1 - side)):
-            older = lanes_from(2 * which + 1 - n, rows)
-            bring(old.at[n, 0], k_s.at[older])
-            bring(old.at[n, 1], v_s.at[older])
-    for slot in range(ROW):
-        part = lambda stream: row_part(streams, theirs, swap, slot, stream, quarter)
-        block = place ^ slot
-        newer = lanes_from(ROW + block, rows)
-        bring(part(0), q_s.at[lanes_from(block, rows)])
-        bring(part(1), k_s.at[newer])
-        bring(part(2), v_s.at[newer])
-    for copy in copies:
-        copy.wait()
-
-    for group in range(ROW // GROUP):
-        tall = GROUP * rows
-        width = (ROW + GROUP * (group + 1)) * rows
-        here = slice(group * tall, (group + 1) * tall)
-        for block in range(GROUP):
-            position = base + (group * GROUP + block) * rows + lax.broadcasted_iota(jnp.int32, (rows, 1), 0)
-            first = contig_start(docs_ref, position)
-            at = base - ROW * rows + lax.broadcasted_iota(jnp.int32, (rows, width), 1)
-            bias_s[block * rows : (block + 1) * rows, 0:width] = jnp.where(
-                (at >= first) & (at <= position), 0.0, -jnp.inf
-            )
-        for head in range(quarter // HEAD):
-            lanes = slice(head * HEAD, (head + 1) * HEAD)
-            turn = head % 2
-            for n in range(0, width, KEYS):
-                tile = slice(n, n + KEYS)
-                s_s[turn, :, tile] = lax.dot_general(
-                    q_s[here, lanes],
-                    k_s[tile, lanes],
-                    (((1,), (1,)), ((), ())),
-                    preferred_element_type=F32,
+    part = functools.partial(row_part, streams, theirs, swap, quarter=quarter)
+
+    def run(first_pair, second_pair):
+        for group, (asking, seen) in enumerate(((first_pair, first_pair), (second_pair, (0, 1, 2, 3)))):
+            starts = [base + (2 * (side if old else 1 - side) + 1 - n - ROW) * rows for old in (1, 0) for n in (0, 1)]
+            starts += [base + (place ^ slot) * rows for slot in seen]
+            for at, slot in enumerate(asking):
+                position = base + (place ^ slot) * rows + lax.broadcasted_iota(jnp.int32, (rows, 1), 0)
+                first = contig_start(docs_ref, position)
+                for n, start in enumerate(starts):
+                    token = start + lax.broadcasted_iota(jnp.int32, (rows, rows), 1)
+                    bias_s[group, at * rows : (at + 1) * rows, n * rows : (n + 1) * rows] = jnp.where(
+                        (token >= first) & (token <= position), 0.0, -jnp.inf
+                    )
+            for head in range(quarter // HEAD):
+                lanes = slice(head * HEAD, (head + 1) * HEAD)
+                olds = lambda kind: [old[n, kind, :, lanes] for old in (own, cross) for n in (0, 1)]
+
+                def keep(m, top, below):
+                    out = slice(asking[0] * rows + m, asking[0] * rows + m + CHUNK)
+                    m_ref[out, lanes] = top
+                    l_ref[out, lanes] = below
+
+                acc_ref[asking[0] * rows : (asking[1] + 1) * rows, lanes] = softmax_group(
+                    jnp.concatenate([part(slot, 0, head) for slot in asking], axis=0),
+                    olds(0) + [part(slot, 1, head) for slot in seen],
+                    olds(1) + [part(slot, 2, head) for slot in seen],
+                    bias_s.at[group],
+                    head % 2,
+                    s_s,
+                    p_s,
+                    keep,
                 )
-            for m in range(0, tall, CHUNK):
-                some = slice(m, m + CHUNK)
-                out = slice(group * tall + m, group * tall + m + CHUNK)
-                top = None
-                parts = []
-                for n in range(0, width, LANES):
-                    part = s_s[turn, some, n : n + LANES] + bias_s[some, n : n + LANES]
-                    parts.append(part)
-                    top = part if top is None else jnp.maximum(top, part)
-                top = jnp.broadcast_to(jnp.max(top, axis=1, keepdims=True), (CHUNK, LANES))
-                m_ref[out, lanes] = top
-                below = jnp.zeros((CHUNK, LANES), F32)
-                for n, part in enumerate(parts):
-                    weight = jnp.exp2((part - top) * SCALE)
-                    below = below + weight
-                    p_s[turn, some, n * LANES : (n + 1) * LANES] = weight.astype(BF16)
-                l_ref[out, lanes] = jnp.broadcast_to(jnp.sum(below, axis=1, keepdims=True), (CHUNK, LANES))
-            acc_ref[here, lanes] = jnp.dot(
-                p_s[turn, :, 0:width], v_s[0:width, lanes], preferred_element_type=F32
-            )
+
+    @pl.when(side == 0)
+    def _():
+        run((0, 1), (2, 3))
+
+    @pl.when(side == 1)
+    def _():
+        run((2, 3), (0, 1))
 
 
 def attend(doc_lengths, streams, theirs, swap, own, cross):
@@ -535,20 +542,16 @@
     heads = quarter // HEAD
     return pl.pallas_call(
         attend_body,
-        in_specs=[SMEM] + [ANY] * 5,
+        in_specs=[SMEM] + [VMEM] * 5,
         out_specs=[VMEM] * 3,
         out_shape=[
             jax.ShapeDtypeStruct((ROW * rows, quarter), F32),
         ]
         * 3,
         scratch_shapes=[
-            pltpu.VMEM((ROW * rows, quarter), BF16),
-            pltpu.VMEM((2 * ROW * rows, quarter), BF16),
-            pltpu.VMEM((2 * ROW * rows, quarter), BF16),
-            pltpu.VMEM((GROUP * rows, 2 * ROW * rows), F32),
-            pltpu.VMEM((2, GROUP * rows, 2 * ROW * rows), F32),
-            pltpu.VMEM((2, GROUP * rows, 2 * ROW * rows), BF16),
-            pltpu.SemaphoreType.DMA((5 * ROW,)),
+            pltpu.VMEM((2, 2 * rows, 2 * ROW * rows), F32),
+            pltpu.VMEM((2, 2 * rows, 2 * ROW * rows), F32),
+            pltpu.VMEM((2, 2 * rows, 2 * ROW * rows), BF16),
         ],
         compiler_params=limits(20),
         cost_estimate=cost(26 * 4 * rows * rows * quarter, 14 * ROW * rows * quarter, 26 * heads * rows * rows),
@@ -557,76 +560,60 @@
 
 
 def attend_last_body(docs_ref, streams, theirs, swap, *refs):
-    olds, (acc_ref, m_ref, l_ref), outs, (q_s, kv_s, o_s, sems) = refs[:4], refs[4:7], refs[7:11], refs[11:]
+    cross_l, own_s, own_l, cross_s, acc_ref, m_ref, l_ref = refs[:7]
+    outs = refs[7:]
     _, side, place, row = spot()
-    rows, quarter = q_s.shape[1:]
+    rows, quarter = acc_ref.shape[0] // ROW, acc_ref.shape[1]
     base = row * (ROW * rows)
-    copies = []
-
-    def copy_of(source, target, n):
-        return pltpu.make_async_copy(source, target, sems.at[n])
-
-    for slot in range(ROW):
-        copies.append(copy_of(row_part(streams, theirs, swap, slot, 0, quarter), q_s.at[place ^ slot], slot))
-        copies[-1].start()
-    for which in range(2):
-        large, small = olds[2 * which : 2 * which + 2]
-        arrived = [
-            copy_of(small.at[0], kv_s.at[0], ROW),
-            copy_of(large.at[1], kv_s.at[1], ROW + 1),
-            copy_of(large.at[0], kv_s.at[2], ROW + 2),
-        ]
-
-        @pl.when(side == which)
-        def _():
-            for copy in arrived:
-                copy.start()
-
-    for copy in copies + arrived:
-        copy.wait()
-    heads = [slice(n, n + HEAD) for n in range(0, quarter, HEAD)]
-    for block in range(ROW):
-        slot = place ^ block
-        here = slice(block * rows, (block + 1) * rows)
-        seen = ROW - 1 - block
-        width = seen * rows
-        if not seen:
-            for lanes in heads:
-                o_s[slot, :, lanes] = (acc_ref[here, lanes] * (1.0 / l_ref[here, lanes])).astype(BF16)
-            continue
-        position = base + block * rows + lax.broadcasted_iota(jnp.int32, (rows, 1), 0)
-        first = contig_start(docs_ref, position)
-        at = base - (ROW + seen) * rows + lax.broadcasted_iota(jnp.int32, (rows, width), 1)
-        allowed = at >= first
-        scores = [
-            lax.dot_general(
-                q_s[block, :, lanes],
-                kv_s[block : ROW - 1, 0, :, lanes].reshape(width, HEAD),
-                (((1,), (1,)), ((), ())),
-                preferred_element_type=F32,
-            )
-            for lanes in heads
-        ]
-        scores = [jnp.where(allowed, score, -jnp.inf) for score in scores]
-        tops = [
-            jnp.maximum(m_ref[here, lanes], jnp.max(score, axis=1, keepdims=True))
-            for lanes, score in zip(heads, scores)
-        ]
-        weights = [
-            jnp.exp2((score - jnp.concatenate([top] * seen, axis=1)) * SCALE)
-            for score, top in zip(scores, tops)
-        ]
-        for lanes, top, weight in zip(heads, tops, weights):
-            fade = jnp.exp2((m_ref[here, lanes] - top) * SCALE)
-            share = 1.0 / (l_ref[here, lanes] * fade + jnp.sum(weight, axis=1, keepdims=True))
-            more = jnp.dot(
-                weight.astype(BF16),
-                kv_s[block : ROW - 1, 1, :, lanes].reshape(width, HEAD),
-                preferred_element_type=F32,
-            )
-            o_s[slot, :, lanes] = ((acc_ref[here, lanes] * fade + more) * share).astype(BF16)
-    for slot, out in enumerate(outs):
-        out[...] = o_s[slot]
+    heads = range(quarter // HEAD)
+
+    def run(early, late, large, small):
+        for asking, blocks in ((early, ((small, 0), (large, 1), (large, 0))), (late, ((large, 0),))):
+            width = len(blocks) * rows
+            here = slice(asking[0] * rows, (asking[1] + 1) * rows)
+            token = base - (ROW + len(blocks)) * rows + lax.broadcasted_iota(jnp.int32, (rows, width), 1)
+            allowed = []
+            for slot in asking:
+                position = base + (place ^ slot) * rows + lax.broadcasted_iota(jnp.int32, (rows, 1), 0)
+                allowed.append((token >= contig_start(docs_ref, position)).astype(jnp.int32))
+            allowed = jnp.concatenate(allowed, axis=0) != 0
+            lanes_of = [slice(head * HEAD, (head + 1) * HEAD) for head in heads]
+            stack = lambda kind, lanes: jnp.concatenate([ref[n, kind, :, lanes] for ref, n in blocks], axis=0)
+            scores = [
+                lax.dot_general(
+                    jnp.concatenate(
+                        [row_part(streams, theirs, swap, slot, 0, head, quarter) for slot in asking], axis=0
+                    ),
+                    stack(0, lanes_of[head]),
+                    (((1,), (1,)), ((), ())),
+                    preferred_element_type=F32,
+                )
+                for head in heads
+            ]
+            scores = [jnp.where(allowed, score, -jnp.inf) for score in scores]
+            tops = [
+                jnp.maximum(m_ref[here, lanes], jnp.max(score, axis=1, keepdims=True))
+                for lanes, score in zip(lanes_of, scores)
+            ]
+            weights = [
+                jnp.exp2((score - jnp.concatenate([top] * len(blocks), axis=1)) * SCALE)
+                for score, top in zip(scores, tops)
+            ]
+            for lanes, top, weight in zip(lanes_of, tops, weights):
+                fade = jnp.exp2((m_ref[here, lanes] - top) * SCALE)
+                share = 1.0 / (l_ref[here, lanes] * fade + jnp.sum(weight, axis=1, keepdims=True))
+                more = jnp.dot(weight.astype(BF16), stack(1, lanes), preferred_element_type=F32)
+                made = ((acc_ref[here, lanes] * fade + more) * share).astype(BF16)
+                for n, slot in enumerate(asking):
+                    outs[slot][:, lanes] = made[n * rows : (n + 1) * rows]
+
+    @pl.when(side == 0)
+    def _():
+        run((0, 1), (2, 3), cross_l, own_s)
+
+    @pl.when(side == 1)
+    def _():
+        run((2, 3), (0, 1), own_l, cross_s)
 
 
 def attend_last(doc_lengths, streams, theirs, swap, olds, acc, top, below):
@@ -634,15 +621,9 @@
     heads = quarter // HEAD
     return pl.pallas_call(
         attend_last_body,
-        in_specs=[SMEM] + [ANY] * 7 + [VMEM] * 3,
+        in_specs=[SMEM] + [VMEM] * 10,
         out_specs=[VMEM] * ROW,
         out_shape=[jax.ShapeDtypeStruct((rows, quarter), BF16)] * ROW,
-        scratch_shapes=[
-            pltpu.VMEM((ROW, rows, quarter), BF16),
-            pltpu.VMEM((ROW - 1, 2, rows, quarter), BF16),
-            pltpu.VMEM((ROW, rows, quarter), BF16),
-            pltpu.SemaphoreType.DMA((2 * ROW,)),
-        ],
         compiler_params=limits(16),
         cost_estimate=cost(6 * 4 * rows * rows * quarter, 12 * ROW * rows * quarter, 6 * heads * rows * rows),
         name="attend_last",

time: 87 us -> 81.5 us (0.937)
  Pallas kernels: 24.7 us -> 19.2 us
    pallas_call x2, Pallas kernels: 9.8 us -> 6.96 us  [the longest x1 4.85 us: attend(): pl.pallas_call(attend_body, in_specs=[SMEM] + [VMEM] * 5, out_specs=[VMEM...]
    pallas_call x1, Pallas kernels: 4.99 us -> 2.32 us  [hyena_ends(): pl.pallas_call(functools.partial(hyena_ends_body, filters), grid=(STEPS,)...]
  transfers between devices with their start and end apart: 17 -> 17, of which waited for: 6 -> 6; matrix products, arithmetic and copies ran while one was open for 0% -> 0% of each run, Pallas kernels for 26% -> 21%
where the time goes in v2:
time: 81.5 us; the launch traced here: 81.2 us
  starting transfers between devices  38.8 us (48%)
  waiting for transfers between devices  22.2 us (27%)
  Pallas kernels  19.2 us (24%)
  between operations  0.96 us (1%)
    ppermute x9, starting transfers between devices, ahead(): return lax.ppermute(value, axis, pairs)  31.8 us
    ppermute x9, waiting for transfers between devices, ahead(): return lax.ppermute(value, axis, pairs)  16.6 us
    ppermute x8, starting transfers between devices, flip(): return lax.ppermute(value, axis, [(at, at ^ bit) for at in range(count)])  6.99 us
    ppermute x8, waiting for transfers between devices, flip(): return lax.ppermute(value, axis, [(at, at ^ bit) for at in range(count)])  5.58 us
    pallas_call x1, Pallas kernels, attend(): pl.pallas_call(attend_body, in_specs=[SMEM] + [VMEM] * 5, out_specs=[VMEM...  4.85 us
    pallas_call x1, Pallas kernels, hyena_near(): pl.pallas_call(functools.partial(hyena_near_body, filters), grid=(STEPS,)...  4.34 us
    pallas_call x1, Pallas kernels, hyena_finish(): pl.pallas_call(functools.partial(hyena_out_body, filters), grid=(STEPS,),...  3.17 us
    pallas_call x1, Pallas kernels, hyena_ends(): pl.pallas_call(functools.partial(hyena_ends_body, filters), grid=(STEPS,)...  2.32 us
  transfers between devices with their start and end apart: 17, of which 6 were waited for; matrix products, arithmetic and copies ran while one was open for 0% of the time, Pallas kernels for 21%

profile of v2, /device:TPU:0, one launch (start us, length us, event | category | flops | bytes accessed | tf_op | source)
XLA Modules:
  0.0 81.2 jit_solution(9379289182097999884)
XLA Ops:
  0.6 1.3 %front.1 = (bf16[3,128,1024]{2,1,0:T(8,128)(2,1)S(1)}, bf16[3,8,2048]{2,1,0:T(8,128)(2,1)S(1)}) custom-call(bf16[3,128,2048]{2,1,0:T(8,128)(2,1)} %bitcast.4, bf16[3,128,2048]{2,1,0:T(8,128)(2,1)} %bitcast.9), custom_call_target="tpu_custom_call" | custom-call | bytes 1572864 | tf_op jit(solution)/shard_map/front/pallas_call | solution.py:378
  1.9 0.6 collective-permute-start.6
  2.5 1.9 %collective-permute-done.6.theirs_ref.theirs = bf16[3,128,1024]{2,1,0:T(8,128)(2,1)S(1)} collective-permute-done((bf16[3,128,1024]{2,1,0:T(8,128)(2,1)S(1)}, bf16[3,128,1024]{2,1,0:T(8,128)(2,1)S(1)}, u32[]{:S(2)}, u32[]{:S(2)}) %collective-permute-start.6) | collective-permute-done | bytes 786464 | tf_op jit(solution)/shard_map/ppermute | solution.py:23
  4.4 0.1 pack.3
  4.5 4.9 %collective-permute-start.10 = (bf16[2,2,128,512]{3,2,1,0:T(8,128)(2,1)S(1)}, bf16[2,2,128,512]{3,2,1,0:T(8,128)(2,1)S(1)}, u32[]{:S(2)}, u32[]{:S(2)}) collective-permute-start(bf16[2,2,128,512]{3,2,1,0:T(8,128)(2,1)S(1)} %get-tuple-element.38), channel_id=1, source_target_pairs={{0,4},{1,5},{2,6},{3,7},{4,8},{5,9},{6,10},{7,11},{8,12},{9,13},{1... | collective-permute-start | bytes 1572872 | tf_op jit(solution)/shard_map/ppermute | solution.py:37
  9.4 4.6 %collective-permute-start.8 = (bf16[2,2,128,512]{3,2,1,0:T(8,128)(2,1)S(1)}, bf16[2,2,128,512]{3,2,1,0:T(8,128)(2,1)S(1)}, u32[]{:S(2)}, u32[]{:S(2)}) collective-permute-start(bf16[2,2,128,512]{3,2,1,0:T(8,128)(2,1)S(1)} %get-tuple-element.37), channel_id=1, source_target_pairs={{0,6},{1,7},{2,4},{3,5},{4,10},{5,11},{6,8},{7,9},{8,14},{9,15},{1... | collective-permute-start | bytes 1572872 | tf_op jit(solution)/shard_map/ppermute | solution.py:37
  14.0 0.1 pack.2
  14.1 0.6 collective-permute-start.7
  14.6 1.3 %collective-permute-start = (bf16[3,8,2048]{2,1,0:T(8,128)(2,1)S(1)}, bf16[3,8,2048]{2,1,0:T(8,128)(2,1)S(1)}, u32[]{:S(2)}, u32[]{:S(2)}) collective-permute-start(bf16[3,8,2048]{2,1,0:T(8,128)(2,1)S(1)} %get-tuple-element.24), channel_id=1, source_target_pairs={{0,1},{1,2},{2,3},{3,4},{4,5},{5,6},{6,7},{7,8},{8,9},{9,10},{10,1... | collective-permute-start | bytes 294920 | tf_op jit(solution)/shard_map/ppermute | solution.py:37
  15.9 5.7 %collective-permute-done.10.pairs.own = bf16[2,2,128,512]{3,2,1,0:T(8,128)(2,1)S(1)} collective-permute-done((bf16[2,2,128,512]{3,2,1,0:T(8,128)(2,1)S(1)}, bf16[2,2,128,512]{3,2,1,0:T(8,128)(2,1)S(1)}, u32[]{:S(2)}, u32[]{:S(2)}) %collective-permute-start.10) | collective-permute-done | bytes 524320 | tf_op jit(solution)/shard_map/ppermute | solution.py:37
  21.6 0.7 collective-permute-start.12
  22.3 9.8 %collective-permute-done.8.pairs.cross = bf16[2,2,128,512]{3,2,1,0:T(8,128)(2,1)S(1)} collective-permute-done((bf16[2,2,128,512]{3,2,1,0:T(8,128)(2,1)S(1)}, bf16[2,2,128,512]{3,2,1,0:T(8,128)(2,1)S(1)}, u32[]{:S(2)}, u32[]{:S(2)}) %collective-permute-start.8) | collective-permute-done | bytes 524320 | tf_op jit(solution)/shard_map/ppermute | solution.py:37
  32.1 0.7 collective-permute-start.9
  32.8 2.3 %hyena_ends.1 = (bf16[128,2048]{1,0:T(8,128)(2,1)S(1)}, f32[16,1024]{1,0:T(8,128)S(1)}, f32[16,1024]{1,0:T(8,128)S(1)}, f32[16,1024]{1,0:T(8,128)S(1)}, f32[16,1024]{1,0:T(8,128)S(1)}) custom-call(bf16[3,128,2048]{2,1,0:T(8,128)(2,1)S(1)} %bitcast.10, bf16[3,8,2048]{2,1,0:T(8,128)(2,1)S(1)} %collective-permute-done.halo_ref, f32[3,3,2048]{2,1,0:T(4,128)S(1)} %copy-done.2, ...), custom_call_target="tpu_custom_call" | custom-call | flops 134217728 | bytes 2097152 | tf_op jit(solution)/shard_map/hyena_ends/pallas_call | solution.py:154
  35.2 0.1 collective-permute-start.1
  35.2 1.2 %collective-permute-done.1.refs_1_ = f32[16,1024]{1,0:T(8,128)S(1)} collective-permute-done((f32[16,1024]{1,0:T(8,128)S(1)}, f32[16,1024]{1,0:T(8,128)S(1)}, u32[]{:S(2)}, u32[]{:S(2)}) %collective-permute-start.1) | collective-permute-done | bytes 65568 | tf_op jit(solution)/shard_map/ppermute | solution.py:23
  36.5 2.4 %collective-permute-start.2 = (f32[16,1024]{1,0:T(8,128)S(1)}, f32[16,1024]{1,0:T(8,128)S(1)}, u32[]{:S(2)}, u32[]{:S(2)}) collective-permute-start(f32[16,1024]{1,0:T(8,128)S(1)} %get-tuple-element.29.refs_0_), channel_id=1, source_target_pairs={{0,2},{1,3},{2,0},{3,1},{4,6},{5,7},{6,4},{7,5},{8,10},{9,11},{10,... | collective-permute-start | bytes 196616 | tf_op jit(solution)/shard_map/ppermute | solution.py:23
  38.9 2.4 %collective-permute-done.2.refs_1_ = f32[16,1024]{1,0:T(8,128)S(1)} collective-permute-done((f32[16,1024]{1,0:T(8,128)S(1)}, f32[16,1024]{1,0:T(8,128)S(1)}, u32[]{:S(2)}, u32[]{:S(2)}) %collective-permute-start.2) | collective-permute-done | bytes 65568 | tf_op jit(solution)/shard_map/ppermute | solution.py:23
  41.4 13.9 %collective-permute-start.3 = (f32[16,1024]{1,0:T(8,128)S(1)}, f32[16,1024]{1,0:T(8,128)S(1)}, u32[]{:S(2)}, u32[]{:S(2)}) collective-permute-start(f32[16,1024]{1,0:T(8,128)S(1)} %get-tuple-element.30.refs_0_), channel_id=1, source_target_pairs={{0,4},{1,5},{2,6},{3,7},{4,8},{5,9},{6,10},{7,11},{8,12},{9,13},{1... | collective-permute-start | bytes 196616 | tf_op jit(solution)/shard_map/ppermute | solution.py:37
  55.3 0.7 collective-permute-start.11
  56.0 1.1 %collective-permute-done.3.refs_1_.refs_0_ = f32[16,1024]{1,0:T(8,128)S(1)} collective-permute-done((f32[16,1024]{1,0:T(8,128)S(1)}, f32[16,1024]{1,0:T(8,128)S(1)}, u32[]{:S(2)}, u32[]{:S(2)}) %collective-permute-start.3) | collective-permute-done | bytes 65568 | tf_op jit(solution)/shard_map/ppermute | solution.py:37
  57.2 0.7 collective-permute-start.13
  57.9 4.5 %collective-permute-start.4 = (f32[16,1024]{1,0:T(8,128)S(1)}, f32[16,1024]{1,0:T(8,128)S(1)}, u32[]{:S(2)}, u32[]{:S(2)}) collective-permute-start(f32[16,1024]{1,0:T(8,128)S(1)} %shard_map.79), channel_id=1, source_target_pairs={{0,8},{1,9},{2,10},{3,11},{4,12},{5,13},{6,14},{7,15},{16,24},{17,... | collective-permute-start | bytes 196616 | tf_op jit(solution)/shard_map/ppermute | solution.py:37
  62.3 4.9 %attend.1 = (f32[512,512]{1,0:T(8,128)S(1)}, f32[512,512]{1,0:T(8,128)S(1)}, f32[512,512]{1,0:T(8,128)S(1)}) custom-call(s32[4]{0:T(128)S(1)} %copy-done.5, bf16[3,128,2048]{2,1,0:T(8,128)(2,1)S(1)} %bitcast.7, bf16[3,128,1024]{2,1,0:T(8,128)(2,1)S(1)} %collective-permute-done.6.theirs_ref.theirs, bf16[2,3,128,512]{3,2,1,0:T(8,128)(2,1)S(1)} %collective-permute-done.7.swap, ...), custom_call_target="tpu_custom_call" | custom-call | flops 872415232 | bytes 3670016 | tf_op jit(solution)/shard_map/attend/pallas_call | solution.py:543
  67.2 2.1 %attend_last.1 = (bf16[128,512]{1,0:T(8,128)(2,1)S(1)}, bf16[128,512]{1,0:T(8,128)(2,1)S(1)}, bf16[128,512]{1,0:T(8,128)(2,1)S(1)}, bf16[128,512]{1,0:T(8,128)(2,1)S(1)}) custom-call(s32[4]{0:T(128)S(1)} %copy-done.5, bf16[3,128,2048]{2,1,0:T(8,128)(2,1)S(1)} %bitcast.8, bf16[3,128,1024]{2,1,0:T(8,128)(2,1)S(1)} %collective-permute-done.6.theirs_ref.theirs, ...), custom_call_target="tpu_custom_call" | custom-call | flops 201326592 | bytes 3145728 | tf_op jit(solution)/shard_map/attend_last/pallas_call | solution.py:622
  69.4 0.1 collective-permute-start.14
  69.4 3.1 %collective-permute-start.15 = (bf16[128,512]{1,0:T(8,128)(2,1)S(1)}, bf16[128,512]{1,0:T(8,128)(2,1)S(1)}, u32[]{:S(2)}, u32[]{:S(2)}) collective-permute-start(bf16[128,512]{1,0:T(8,128)(2,1)S(1)} %get-tuple-element.44), channel_id=1, source_target_pairs={{0,2},{1,3},{2,0},{3,1},{4,6},{5,7},{6,4},{7,5},{8,10},{9,11},{10,... | collective-permute-start | bytes 393224 | tf_op jit(solution)/shard_map/ppermute | solution.py:23
  72.5 0.1 shard_map.80
  72.6 0.2 collective-permute-start.5
  72.8 4.3 %hyena_near.1.near_ref = f32[128,2048]{1,0:T(8,128)S(1)} custom-call(bf16[128,2048]{1,0:T(8,128)(2,1)S(1)} %get-tuple-element.25.mixed_ref, f32[16,128]{1,0:T(8,128)S(1)} %bitcast.13, f32[16,128]{1,0:T(8,128)S(1)} %bitcast.16), custom_call_target="tpu_custom_call" | custom-call | flops 536870912 | bytes 3145728 | tf_op jit(solution)/shard_map/hyena_near/pallas_call | solution.py:211
  77.2 3.2 %hyena_finish.1 = bf16[128,2048]{1,0:T(8,128)(2,1)} custom-call(f32[128,2048]{1,0:T(8,128)S(1)} %hyena_near.1.near_ref, bf16[3,128,2048]{2,1,0:T(8,128)(2,1)S(1)} %bitcast.11, bf16[3,8,2048]{2,1,0:T(8,128)(2,1)S(1)} %collective-permute-done.halo_ref, f32[3,3,2048]{2,1,0:T(4,128)S(1)} %copy-done.2, f32[16,1024]{1,0:T(8,128)S(1)} %get-tuple-element.34.keep_ref, ...), custom_call_target="tpu_custom_call" | custom-call | flops 201326592 | bytes 2621440 | tf_op jit(solution)/shard_map/hyena_finish/pallas_call | solution.py:270
  80.4 0.8 %assemble.1 = bf16[128,2048]{1,0:T(8,128)(2,1)} custom-call(bf16[128,512]{1,0:T(8,128)(2,1)S(1)} %get-tuple-element.42.refs_0_, bf16[128,512]{1,0:T(8,128)(2,1)S(1)} %collective-permute-done.14.refs_1_, bf16[128,512]{1,0:T(8,128)(2,1)S(1)} %collective-permute-done.15.refs_2_, bf16[128,512]{1,0:T(8,128)(2,1)S(1)} %collective-permute-done.16.refs_3_), custom_call_target="tpu_custom_call" | custom-call | bytes 1048576 | tf_op jit(solution)/shard_map/assemble/pallas_call | solution.py:645
  (29 shorter events, 0.2 us)
Async XLA Ops:
  0.6 3.8 %copy-start = (bf16[128,3,2048]{2,0,1:T(8,128)(2,1)S(1)}, bf16[128,3,2048]{2,0,1:T(8,128)(2,1)}, u32[]{:S(2)}) copy-start(bf16[128,3,2048]{2,0,1:T(8,128)(2,1)} %param.10) | copy-start | bytes 4718596
  1.9 2.5 %collective-permute-start.6 = (bf16[3,128,1024]{2,1,0:T(8,128)(2,1)S(1)}, bf16[3,128,1024]{2,1,0:T(8,128)(2,1)S(1)}, u32[]{:S(2)}, u32[]{:S(2)}) collective-permute-start(bf16[3,128,1024]{2,1,0:T(8,128)(2,1)S(1)} %get-tuple-element.36), channel_id=1, source_target_pairs={{0,1},{1,0},{2,3},{3,2},{4,5},{5,4},{6,7},{7,6},{8,9},{9,8},{10,11... | collective-permute-start | bytes 2359304 | tf_op jit(solution)/shard_map/ppermute | solution.py:23
  4.5 17.1 %collective-permute-start.10 = (bf16[2,2,128,512]{3,2,1,0:T(8,128)(2,1)S(1)}, bf16[2,2,128,512]{3,2,1,0:T(8,128)(2,1)S(1)}, u32[]{:S(2)}, u32[]{:S(2)}) collective-permute-start(bf16[2,2,128,512]{3,2,1,0:T(8,128)(2,1)S(1)} %get-tuple-element.38), channel_id=1, source_target_pairs={{0,4},{1,5},{2,6},{3,7},{4,8},{5,9},{6,10},{7,11},{8,12},{9,13},{1... | collective-permute-start | bytes 1572872 | tf_op jit(solution)/shard_map/ppermute | solution.py:37
  9.4 23.4 %copy-start.1 = (bf16[128,3,2048]{2,0,1:T(8,128)(2,1)S(1)}, bf16[128,3,2048]{2,0,1:T(8,128)(2,1)}, u32[]{:S(2)}) copy-start(bf16[128,3,2048]{2,0,1:T(8,128)(2,1)} %param.6) | copy-start | bytes 4718596
  9.4 23.4 %copy-start.2 = (f32[3,3,2048]{2,1,0:T(4,128)S(1)}, f32[3,3,2048]{2,1,0:T(4,128)}, u32[]{:S(2)}) copy-start(f32[3,3,2048]{2,1,0:T(4,128)} %w_ref.3) | copy-start | bytes 221188
  9.4 23.4 %copy-start.3 = (f32[128,16]{0,1:T(8,128)S(1)}, f32[128,16]{0,1:T(8,128)}, u32[]{:S(2)}) copy-start(f32[128,16]{0,1:T(8,128)} %param.8) | copy-start | bytes 24580
  9.4 23.4 %copy-start.4 = (f32[128,16]{0,1:T(8,128)S(1)}, f32[128,16]{0,1:T(8,128)}, u32[]{:S(2)}) copy-start(f32[128,16]{0,1:T(8,128)} %param.9) | copy-start | bytes 24580
  9.4 22.7 %collective-permute-start.8 = (bf16[2,2,128,512]{3,2,1,0:T(8,128)(2,1)S(1)}, bf16[2,2,128,512]{3,2,1,0:T(8,128)(2,1)S(1)}, u32[]{:S(2)}, u32[]{:S(2)}) collective-permute-start(bf16[2,2,128,512]{3,2,1,0:T(8,128)(2,1)S(1)} %get-tuple-element.37), channel_id=1, source_target_pairs={{0,6},{1,7},{2,4},{3,5},{4,10},{5,11},{6,8},{7,9},{8,14},{9,15},{1... | collective-permute-start | bytes 1572872 | tf_op jit(solution)/shard_map/ppermute | solution.py:37
  14.1 43.8 %collective-permute-start.7 = (bf16[2,3,128,512]{3,2,1,0:T(8,128)(2,1)S(1)}, bf16[2,3,128,512]{3,2,1,0:T(8,128)(2,1)S(1)}, u32[]{:S(2)}, u32[]{:S(2)}) collective-permute-start(bf16[2,3,128,512]{3,2,1,0:T(8,128)(2,1)S(1)} %pack.2), channel_id=1, source_target_pairs={{0,2},{1,3},{2,0},{3,1},{4,6},{5,7},{6,4},{7,5},{8,10},{9,11},{10,... | collective-permute-start | bytes 2359304 | tf_op jit(solution)/shard_map/ppermute | solution.py:23
  14.6 18.1 %collective-permute-start = (bf16[3,8,2048]{2,1,0:T(8,128)(2,1)S(1)}, bf16[3,8,2048]{2,1,0:T(8,128)(2,1)S(1)}, u32[]{:S(2)}, u32[]{:S(2)}) collective-permute-start(bf16[3,8,2048]{2,1,0:T(8,128)(2,1)S(1)} %get-tuple-element.24), channel_id=1, source_target_pairs={{0,1},{1,2},{2,3},{3,4},{4,5},{5,6},{6,7},{7,8},{8,9},{9,10},{10,1... | collective-permute-start | bytes 294920 | tf_op jit(solution)/shard_map/ppermute | solution.py:37
  21.6 45.6 %collective-permute-start.12 = (bf16[2,2,128,512]{3,2,1,0:T(8,128)(2,1)S(1)}, bf16[2,2,128,512]{3,2,1,0:T(8,128)(2,1)S(1)}, u32[]{:S(2)}, u32[]{:S(2)}) collective-permute-start(bf16[2,2,128,512]{3,2,1,0:T(8,128)(2,1)S(1)} %collective-permute-done.10.pairs.own), channel_id=1, source_target_pairs={{6,10},{7,11},{10,14},{11,15},{22,26},{23,27},{26,30},{27,31}} | collective-permute-start | bytes 1572872 | tf_op jit(solution)/shard_map/ppermute | solution.py:37
  32.1 35.2 %collective-permute-start.9 = (bf16[2,2,128,512]{3,2,1,0:T(8,128)(2,1)S(1)}, bf16[2,2,128,512]{3,2,1,0:T(8,128)(2,1)S(1)}, u32[]{:S(2)}, u32[]{:S(2)}) collective-permute-start(bf16[2,2,128,512]{3,2,1,0:T(8,128)(2,1)S(1)} %collective-permute-done.8.pairs.cross), channel_id=1, source_target_pairs={{4,8},{5,9},{8,12},{9,13},{20,24},{21,25},{24,28},{25,29}} | collective-permute-start | bytes 1572872 | tf_op jit(solution)/shard_map/ppermute | solution.py:37
  32.8 29.5 %copy-start.5 = (s32[4]{0:T(128)S(1)}, s32[4]{0:T(128)}, u32[]{:S(2)}) copy-start(s32[4]{0:T(128)} %docs_ref.3) | copy-start | bytes 52
  35.2 1.3 %collective-permute-start.1 = (f32[16,1024]{1,0:T(8,128)S(1)}, f32[16,1024]{1,0:T(8,128)S(1)}, u32[]{:S(2)}, u32[]{:S(2)}) collective-permute-start(f32[16,1024]{1,0:T(8,128)S(1)} %get-tuple-element.27), channel_id=1, source_target_pairs={{0,1},{1,0},{2,3},{3,2},{4,5},{5,4},{6,7},{7,6},{8,9},{9,8},{10,11... | collective-permute-start | bytes 196616 | tf_op jit(solution)/shard_map/ppermute | solution.py:23
  36.5 4.8 %collective-permute-start.2 = (f32[16,1024]{1,0:T(8,128)S(1)}, f32[16,1024]{1,0:T(8,128)S(1)}, u32[]{:S(2)}, u32[]{:S(2)}) collective-permute-start(f32[16,1024]{1,0:T(8,128)S(1)} %get-tuple-element.29.refs_0_), channel_id=1, source_target_pairs={{0,2},{1,3},{2,0},{3,1},{4,6},{5,7},{6,4},{7,5},{8,10},{9,11},{10,... | collective-permute-start | bytes 196616 | tf_op jit(solution)/shard_map/ppermute | solution.py:23
  41.4 15.8 %collective-permute-start.3 = (f32[16,1024]{1,0:T(8,128)S(1)}, f32[16,1024]{1,0:T(8,128)S(1)}, u32[]{:S(2)}, u32[]{:S(2)}) collective-permute-start(f32[16,1024]{1,0:T(8,128)S(1)} %get-tuple-element.30.refs_0_), channel_id=1, source_target_pairs={{0,4},{1,5},{2,6},{3,7},{4,8},{5,9},{6,10},{7,11},{8,12},{9,13},{1... | collective-permute-start | bytes 196616 | tf_op jit(solution)/shard_map/ppermute | solution.py:37
  55.3 11.9 %collective-permute-start.11 = (bf16[1,2,128,512]{3,2,1,0:T(8,128)(2,1)S(1)}, bf16[1,2,128,512]{3,2,1,0:T(8,128)(2,1)S(1)}, u32[]{:S(2)}, u32[]{:S(2)}) collective-permute-start(bf16[1,2,128,512]{3,2,1,0:T(8,128)(2,1)S(1)} %odd.2), channel_id=1, source_target_pairs={{4,8},{5,9},{8,12},{9,13},{20,24},{21,25},{24,28},{25,29}} | collective-permute-start | bytes 786440 | tf_op jit(solution)/shard_map/ppermute | solution.py:37
  57.2 10.1 %collective-permute-start.13 = (bf16[1,2,128,512]{3,2,1,0:T(8,128)(2,1)S(1)}, bf16[1,2,128,512]{3,2,1,0:T(8,128)(2,1)S(1)}, u32[]{:S(2)}, u32[]{:S(2)}) collective-permute-start(bf16[1,2,128,512]{3,2,1,0:T(8,128)(2,1)S(1)} %odd.3), channel_id=1, source_target_pairs={{6,10},{7,11},{10,14},{11,15},{22,26},{23,27},{26,30},{27,31}} | collective-permute-start | bytes 786440 | tf_op jit(solution)/shard_map/ppermute | solution.py:37
  57.9 14.7 %collective-permute-start.4 = (f32[16,1024]{1,0:T(8,128)S(1)}, f32[16,1024]{1,0:T(8,128)S(1)}, u32[]{:S(2)}, u32[]{:S(2)}) collective-permute-start(f32[16,1024]{1,0:T(8,128)S(1)} %shard_map.79), channel_id=1, source_target_pairs={{0,8},{1,9},{2,10},{3,11},{4,12},{5,13},{6,14},{7,15},{16,24},{17,... | collective-permute-start | bytes 196616 | tf_op jit(solution)/shard_map/ppermute | solution.py:37
  69.4 11.0 %collective-permute-start.14 = (bf16[128,512]{1,0:T(8,128)(2,1)S(1)}, bf16[128,512]{1,0:T(8,128)(2,1)S(1)}, u32[]{:S(2)}, u32[]{:S(2)}) collective-permute-start(bf16[128,512]{1,0:T(8,128)(2,1)S(1)} %get-tuple-element.43), channel_id=1, source_target_pairs={{0,1},{1,0},{2,3},{3,2},{4,5},{5,4},{6,7},{7,6},{8,9},{9,8},{10,11... | collective-permute-start | bytes 393224 | tf_op jit(solution)/shard_map/ppermute | solution.py:23
  69.4 10.9 %collective-permute-start.15 = (bf16[128,512]{1,0:T(8,128)(2,1)S(1)}, bf16[128,512]{1,0:T(8,128)(2,1)S(1)}, u32[]{:S(2)}, u32[]{:S(2)}) collective-permute-start(bf16[128,512]{1,0:T(8,128)(2,1)S(1)} %get-tuple-element.44), channel_id=1, source_target_pairs={{0,2},{1,3},{2,0},{3,1},{4,6},{5,7},{6,4},{7,5},{8,10},{9,11},{10,... | collective-permute-start | bytes 393224 | tf_op jit(solution)/shard_map/ppermute | solution.py:23
  72.5 7.9 %collective-permute-start.16 = (bf16[128,512]{1,0:T(8,128)(2,1)S(1)}, bf16[128,512]{1,0:T(8,128)(2,1)S(1)}, u32[]{:S(2)}, u32[]{:S(2)}) collective-permute-start(bf16[128,512]{1,0:T(8,128)(2,1)S(1)} %get-tuple-element.45), channel_id=1, source_target_pairs={{0,3},{1,2},{2,1},{3,0},{4,7},{5,6},{6,5},{7,4},{8,11},{9,10},{10,... | collective-permute-start | bytes 393224 | tf_op jit(solution)/shard_map/ppermute | solution.py:23
  72.6 4.6 %collective-permute-start.5 = (f32[16,1024]{1,0:T(8,128)S(1)}, f32[16,1024]{1,0:T(8,128)S(1)}, u32[]{:S(2)}, u32[]{:S(2)}) collective-permute-start(f32[16,1024]{1,0:T(8,128)S(1)} %get-tuple-element.35), channel_id=1, source_target_pairs={{0,1},{1,0},{2,3},{3,2},{4,5},{5,4},{6,7},{7,6},{8,9},{9,8},{10,11... | collective-permute-start | bytes 196616 | tf_op jit(solution)/shard_map/ppermute | solution.py:23
